TPU v7x, 32 devices: a whole 2x2x4 slice. The times are simulated.
32 devices in a mesh: layer: 8 (over z, x), dp: 4 (over y, core).
Axes of the slice: x: 2, y: 2, z: 4, core: 2. Of those that a mesh axis runs over, the one named last changes fastest.
Arguments:
- old_heads: float32 [8, 1024, 512], P('layer', 'dp'), parts along dimension 1, may hold values from -6 to 6
- surrogate: float32 [8, 512, 512], P('layer'), may hold values from -0.25 to 0.25
- norm_gain: float32 [8, 512], P('layer'), may hold values from 0.25 to 1.75
- w_qkv: bfloat16 [8, 512, 1536], P('layer'), may hold values from -16 to 16
- w_out: bfloat16 [8, 512, 512], P('layer'), may hold values from -0.25 to 0.25
- w_up: bfloat16 [8, 512, 2048], P('layer'), may hold values from -0.25 to 0.25
- w_down: bfloat16 [8, 2048, 512], P('layer'), may hold values from -0.125 to 0.125
- lengths: int32 [8], P('dp'), parts along dimension 0, may hold values from 32 to 128
Outputs:
- new_heads: float32 [8, 1024, 512], P('layer', 'dp'), parts along dimension 1
- update_rms: float32 [8, 1024], P('layer', 'dp'), parts along dimension 1
There are 4 independent parts, one for each index of `dp`. A program takes and returns all parts, laid end to end along the dimension named above; an argument that names none is the same for every part. Nothing has to cross between parts.
All inputs are finite; a program needn't handle non-finite values.
Results may differ from a plain program's by a relative error of at most 0.015.
Values sent between devices are 32-bit elements; how exact they have to be, the bound alone decides.
No kernel may reach another device: no remote copies, remote signals or barrier semaphores. Data moves between devices by JAX's collectives and lax.ppermute only.
A program may use at most 128 MiB of HBM per device.

v0:
```python
import math

import jax
import jax.numpy as jnp
from jax import lax
from jax.sharding import PartitionSpec as P

HEAD_DIM = 64
SEQ = 128
FINE = 4


precise = lax.Precision.HIGHEST


def passed_along(block, axis, distance):
    devices = range(lax.axis_size(axis))
    route = [(i - distance, i) for i in devices if i - distance in devices]
    return lax.ppermute(block, axis, route)


def causal_allowed(lengths):
    position = jnp.arange(SEQ, dtype=jnp.int32)
    ordered = position[None, :, None] >= position[None, None, :]
    inside = position[None, None, :] < lengths[:, None, None]
    return ordered & inside


def layer_step(current, gain_row, w_qkv, w_out, w_up, w_down, allowed):
    mean_square = jnp.mean(current * current, axis=1, keepdims=True)
    normed = (current * lax.rsqrt(mean_square + 1e-06) * gain_row).astype(jnp.bfloat16)
    packed = jnp.dot(normed, w_qkv, preferred_element_type=jnp.float32).astype(jnp.bfloat16)
    model_width = normed.shape[1]
    head_count = model_width // HEAD_DIM

    def split_heads(block):
        return block.reshape(-1, SEQ, head_count, HEAD_DIM)

    queries = split_heads(packed[:, :model_width])
    key_heads = split_heads(packed[:, model_width : 2 * model_width])
    values = split_heads(packed[:, 2 * model_width :])
    scores = jnp.einsum(
        "sqhd,skhd->shqk", queries, key_heads, preferred_element_type=jnp.float32
    ) / math.sqrt(HEAD_DIM)
    scores = jnp.where(allowed[:, None], scores, -1e30)
    row_max = jnp.max(scores, axis=-1, keepdims=True)
    exponent = jnp.exp(scores - row_max)
    attention = (exponent / jnp.sum(exponent, axis=-1, keepdims=True)).astype(jnp.bfloat16)
    mixed_heads = jnp.einsum(
        "shqk,skhd->sqhd", attention, values, preferred_element_type=jnp.float32
    )
    mixed_heads = mixed_heads.astype(jnp.bfloat16).reshape(current.shape[0], model_width)
    attended = jnp.dot(mixed_heads, w_out, preferred_element_type=jnp.float32)
    hidden = jax.nn.gelu(
        jnp.dot(normed, w_up, preferred_element_type=jnp.float32), approximate=True
    ).astype(jnp.bfloat16)
    return attended + jnp.dot(hidden, w_down, preferred_element_type=jnp.float32)


def fine_sweep(own_start, gain_row, w_qkv, w_out, w_up, w_down, allowed):
    current = own_start
    for substep in range(FINE):
        current = current + layer_step(current, gain_row, w_qkv, w_out, w_up, w_down, allowed) * (
            1.0 / FINE
        )
    return current


def shards(old_heads, surrogate, norm_gain, w_qkv, w_out, w_up, w_down, lengths):
    allowed = causal_allowed(lengths)
    own_start = old_heads[0]
    fine_end = fine_sweep(own_start, norm_gain[0], w_qkv[0], w_out[0], w_up[0], w_down[0], allowed)
    model_width = own_start.shape[1]
    coarse = 0.9 * jnp.eye(model_width, dtype=jnp.float32) + 0.3 * surrogate[0]
    jump_term = fine_end - jnp.dot(
        own_start, coarse, precision=precise, preferred_element_type=jnp.float32
    )
    position = lax.axis_index("layer")
    is_first = position == 0

    def advance(turn_index, relay_state):
        arrived_head, produced = relay_state
        incoming = passed_along(produced, "layer", 1)

        def apply_map():
            return (
                incoming,
                jnp.dot(incoming, coarse, precision=precise, preferred_element_type=jnp.float32)
                + jump_term,
            )

        def keep_state():
            return (arrived_head, produced)

        return lax.cond(position == turn_index + 1, apply_map, keep_state)

    arrived_head, produced = lax.fori_loop(
        0, lax.axis_size("layer") - 1, advance, (own_start, fine_end)
    )
    received = passed_along(produced, "layer", 1)
    previous = jnp.where(is_first, own_start, received)
    difference = previous - own_start
    change = jnp.sqrt(jnp.mean(difference * difference, axis=1))
    return (produced[None], change[None])


def solution(mesh):
    in_specs = (
        P("layer", "dp", None),
        P("layer", None, None),
        P("layer", None),
        P("layer", None, None),
        P("layer", None, None),
        P("layer", None, None),
        P("layer", None, None),
        P("dp"),
    )
    out_specs = (P("layer", "dp", None), P("layer", "dp"))
    return jax.shard_map(shards, mesh=mesh, in_specs=in_specs, out_specs=out_specs, check_vma=False)
```

profile of v0, /device:TPU:26, one launch (start us, length us, event | category | flops | bytes accessed | tf_op | source)
XLA Modules:
  0.0 192.0 jit_solution(10100512201832895098)
XLA Ops:
  2.0 2.2 %convolution_convert_fusion.3 = bf16[256,1536]{1,0:T(8,128)(2,1)S(1)} fusion(bf16[1,512,1536]{2,1,0:T(8,128)(2,1)} %param.15, f32[1,256,512]{2,1,0:T(8,128)} %param.12, f32[512]{0:T(512)} %bitcast.166, f32[256]{0:T(256)S(1)} %add_rsqrt_fusion.3), kind=kOutput, calls=%fused_computation.12 | convolution fusion | flops 403439616 | bytes 2886656 | tf_op jit(solution)/shard_map/dot_general | solution.py:32
  9.6 2.2 %fusion.113 = bf16[2,128,8,64]{1,3,2,0:T(8,128)(2,1)S(1)} fusion(bf16[2,128,8,64]{3,2,1,0:T(8,128)(2,1)} %reshape.203, f32[2,8,128]{2,1,0:T(8,128)S(1)} %fusion.223, f32[2,8,128,128]{2,3,1,0:T(8,128)} %copy-done.6), kind=kOutput, calls=%fused_computation.99 | convolution fusion | flops 34474112 | bytes 1581056 | tf_op jit(solution)/shard_map/shqk,skhd->sqhd/dot_general | solution.py:49
  13.3 4.1 %multiply_reduce_fusion.2 = (f32[256]{0:T(256)S(1)}, f32[256,512]{1,0:T(8,128)}) fusion(f32[256,512]{1,0:T(8,128)} %fusion.146, bf16[1,2048,512]{2,1,0:T(8,128)(2,1)S(1)} %copy-done, bf16[1,512,2048]{2,1,0:T(8,128)(2,1)} %param.17, f32[1,256,512]{2,1,0:T(8,128)S(1)} %copy-done.2, f32[512]{0:T(512)S(1)} %bitcast.167, f32[256]{0:T(256)S(1)} %add_rsqrt_fusion.3), kind=kOutput, calls=%fused_computation.151 | convolution fusion | flops 1079508736 | bytes 5771264 | tf_op jit(solution)/shard_map/dot_general | solution.py:57
  17.4 2.2 %convolution_convert_fusion.2 = bf16[256,1536]{1,0:T(8,128)(2,1)S(1)} fusion(bf16[1,512,1536]{2,1,0:T(8,128)(2,1)} %param.15, f32[256,512]{1,0:T(8,128)} %get-tuple-element.137, f32[512]{0:T(512)S(1)} %bitcast.168, f32[256]{0:T(256)S(1)} %add_rsqrt_fusion.2), kind=kOutput, calls=%fused_computation.11 | convolution fusion | flops 403439616 | bytes 2886656 | tf_op jit(solution)/shard_map/dot_general | solution.py:32
  25.0 2.0 %fusion.114 = bf16[2,128,8,64]{1,3,2,0:T(8,128)(2,1)S(1)} fusion(bf16[2,128,8,64]{3,2,1,0:T(8,128)(2,1)S(1)} %reshape.206, f32[2,8,128]{2,1,0:T(8,128)S(1)} %fusion.228, f32[2,8,128,128]{2,3,1,0:T(8,128)} %copy-done.7), kind=kOutput, calls=%fused_computation.100 | convolution fusion | flops 34474112 | bytes 1581056 | tf_op jit(solution)/shard_map/shqk,skhd->sqhd/dot_general | solution.py:49
  27.7 4.3 %multiply_reduce_fusion.1 = (f32[256]{0:T(256)S(1)}, f32[256,512]{1,0:T(8,128)}) fusion(f32[256,512]{1,0:T(8,128)} %get-tuple-element.137, f32[256,512]{1,0:T(8,128)S(1)} %fusion.144, bf16[1,2048,512]{2,1,0:T(8,128)(2,1)S(1)} %copy-done, bf16[1,512,2048]{2,1,0:T(8,128)(2,1)} %param.17, f32[512]{0:T(512)S(1)} %bitcast.169, f32[256]{0:T(256)S(1)} %add_rsqrt_fusion.2), kind=kOutput, calls=%fused_computation.148 | convolution fusion | flops 1079508736 | bytes 5771264 | tf_op jit(solution)/shard_map/dot_general | solution.py:57
  31.9 2.2 %convolution_convert_fusion.1 = bf16[256,1536]{1,0:T(8,128)(2,1)S(1)} fusion(bf16[1,512,1536]{2,1,0:T(8,128)(2,1)} %param.15, f32[256,512]{1,0:T(8,128)} %get-tuple-element.139, f32[256]{0:T(256)S(1)} %add_rsqrt_fusion.1, f32[512]{0:T(512)S(1)} %bitcast.170), kind=kOutput, calls=%fused_computation.10 | convolution fusion | flops 403439616 | bytes 2886656 | tf_op jit(solution)/shard_map/dot_general | solution.py:32
  39.5 2.0 %fusion.115 = bf16[2,128,8,64]{1,3,2,0:T(8,128)(2,1)S(1)} fusion(bf16[2,128,8,64]{3,2,1,0:T(8,128)(2,1)S(1)} %reshape.209, f32[2,8,128]{2,1,0:T(8,128)S(1)} %fusion.231, f32[2,8,128,128]{2,3,1,0:T(8,128)} %copy-done.8), kind=kOutput, calls=%fused_computation.101 | convolution fusion | flops 34474112 | bytes 1581056 | tf_op jit(solution)/shard_map/shqk,skhd->sqhd/dot_general | solution.py:49
  42.2 4.5 %multiply_reduce_fusion = (f32[256]{0:T(256)S(1)}, f32[256,512]{1,0:T(8,128)}) fusion(f32[256,512]{1,0:T(8,128)} %get-tuple-element.139, f32[256,512]{1,0:T(8,128)S(1)} %fusion.142, bf16[1,2048,512]{2,1,0:T(8,128)(2,1)S(1)} %copy-done, bf16[1,512,2048]{2,1,0:T(8,128)(2,1)} %param.17, f32[256]{0:T(256)S(1)} %add_rsqrt_fusion.1, f32[512]{0:T(512)S(1)} %bitcast.171), kind=kOutput, calls=%fused_computation.145 | convolution fusion | flops 1079508736 | bytes 5771264 | tf_op jit(solution)/shard_map/dot_general | solution.py:57
  46.6 2.2 %convolution_convert_fusion = bf16[256,1536]{1,0:T(8,128)(2,1)S(1)} fusion(bf16[1,512,1536]{2,1,0:T(8,128)(2,1)} %param.15, f32[256,512]{1,0:T(8,128)} %get-tuple-element.141, f32[256]{0:T(256)S(1)} %add_rsqrt_fusion, f32[512]{0:T(512)S(1)} %bitcast.172), kind=kOutput, calls=%fused_computation.9 | convolution fusion | flops 403439616 | bytes 2886656 | tf_op jit(solution)/shard_map/dot_general | solution.py:32
  54.2 2.0 %fusion.116 = bf16[2,128,8,64]{1,3,2,0:T(8,128)(2,1)S(1)} fusion(bf16[2,128,8,64]{3,2,1,0:T(8,128)(2,1)S(1)} %reshape.212, f32[2,8,128]{2,1,0:T(8,128)S(1)} %fusion.234, f32[2,8,128,128]{2,3,1,0:T(8,128)} %copy-done.5), kind=kOutput, calls=%fused_computation.102 | convolution fusion | flops 34474112 | bytes 1581056 | tf_op jit(solution)/shard_map/shqk,skhd->sqhd/dot_general | solution.py:49
  56.8 4.2 %fusion.101 = f32[256,512]{1,0:T(8,128)} fusion(f32[256,512]{1,0:T(8,128)} %get-tuple-element.141, f32[256,512]{1,0:T(8,128)S(1)} %fusion.140, bf16[1,2048,512]{2,1,0:T(8,128)(2,1)S(1)} %copy-done, bf16[1,512,2048]{2,1,0:T(8,128)(2,1)} %param.17, f32[256]{0:T(256)S(1)} %add_rsqrt_fusion, f32[512]{0:T(512)S(1)} %bitcast.173), kind=kOutput, calls=%fused_computation.91 | convolution fusion | flops 1079246848 | bytes 5770240 | tf_op jit(solution)/shard_map/dot_general | solution.py:57
  62.9 2.0 %fusion.100 = f32[256,512]{1,0:T(8,128)} fusion(f32[256,512]{1,0:T(8,128)S(1)} %copy-done.9, f32[1,512,512]{2,1,0:T(8,128)S(1)} %copy-done.4, f32[1,256,512]{2,1,0:T(8,128)S(1)} %copy-done.3), kind=kOutput, calls=%fused_computation.90 | convolution fusion | flops 806486016 | bytes 2621440 | tf_op jit(solution)/shard_map/dot_general | solution.py:75
  64.9 113.9 %while.16 = (s32[]{:T(128)}, f32[256,512]{1,0:T(8,128)}, s32[]{:T(128)}, f32[512,512]{1,0:T(8,128)S(1)}, f32[256,512]{1,0:T(8,128)}, /*index=5*/s32[]{:T(128)}) while((s32[]{:T(128)}, f32[256,512]{1,0:T(8,128)}, s32[]{:T(128)}, f32[512,512]{1,0:T(8,128)S(1)}, f32[256,512]{1,0:T(8,128)}, /*index=5*/s32[]{:T(128)}) %tuple.55), condition=%wide.region_15.16_spmd, body=%wide.region_12.15_spmd.sunk | while | flops 805437440 | bytes 4718747 | solution.py:97
  66.2 14.6 %collective-permute-done = f32[256,512]{1,0:T(8,128)} collective-permute-done((f32[256,512]{1,0:T(8,128)}, f32[256,512]{1,0:T(8,128)}, u32[]{:S(2)}, u32[]{:S(2)}) %collective-permute-start) | collective-permute-done | bytes 524320 | tf_op jit(solution)/shard_map/while/body/eval_jaxpr/ppermute | solution.py:19
  82.0 13.7 %collective-permute-done = f32[256,512]{1,0:T(8,128)} collective-permute-done((f32[256,512]{1,0:T(8,128)}, f32[256,512]{1,0:T(8,128)}, u32[]{:S(2)}, u32[]{:S(2)}) %collective-permute-start) | collective-permute-done | bytes 524320 | tf_op jit(solution)/shard_map/while/body/eval_jaxpr/ppermute | solution.py:19
  97.0 13.5 %collective-permute-done = f32[256,512]{1,0:T(8,128)} collective-permute-done((f32[256,512]{1,0:T(8,128)}, f32[256,512]{1,0:T(8,128)}, u32[]{:S(2)}, u32[]{:S(2)}) %collective-permute-start) | collective-permute-done | bytes 524320 | tf_op jit(solution)/shard_map/while/body/eval_jaxpr/ppermute | solution.py:19
  111.8 12.9 %collective-permute-done = f32[256,512]{1,0:T(8,128)} collective-permute-done((f32[256,512]{1,0:T(8,128)}, f32[256,512]{1,0:T(8,128)}, u32[]{:S(2)}, u32[]{:S(2)}) %collective-permute-start) | collective-permute-done | bytes 524320 | tf_op jit(solution)/shard_map/while/body/eval_jaxpr/ppermute | solution.py:19
  126.0 12.0 %collective-permute-done = f32[256,512]{1,0:T(8,128)} collective-permute-done((f32[256,512]{1,0:T(8,128)}, f32[256,512]{1,0:T(8,128)}, u32[]{:S(2)}, u32[]{:S(2)}) %collective-permute-start) | collective-permute-done | bytes 524320 | tf_op jit(solution)/shard_map/while/body/eval_jaxpr/ppermute | solution.py:19
  139.3 11.2 %collective-permute-done = f32[256,512]{1,0:T(8,128)} collective-permute-done((f32[256,512]{1,0:T(8,128)}, f32[256,512]{1,0:T(8,128)}, u32[]{:S(2)}, u32[]{:S(2)}) %collective-permute-start) | collective-permute-done | bytes 524320 | tf_op jit(solution)/shard_map/while/body/eval_jaxpr/ppermute | solution.py:19
  151.8 23.9 %collective-permute-done = f32[256,512]{1,0:T(8,128)} collective-permute-done((f32[256,512]{1,0:T(8,128)}, f32[256,512]{1,0:T(8,128)}, u32[]{:S(2)}, u32[]{:S(2)}) %collective-permute-start) | collective-permute-done | bytes 524320 | tf_op jit(solution)/shard_map/while/body/eval_jaxpr/ppermute | solution.py:19
  175.8 3.0 %conditional.2 = (f32[256,512]{1,0:T(8,128)}) conditional(s32[]{:T(128)} %convert_element_type.176, f32[256,512]{1,0:T(8,128)} %get-tuple-element.180, (f32[256,512]{1,0:T(8,128)}, f32[512,512]{1,0:T(8,128)S(1)}, f32[256,512]{1,0:T(8,128)}) %tuple.54), branch_computations={%region_13.13_spmd, %region_14.14_spmd} | conditional | flops 805437440 | bytes 2621448 | solution.py:95
  175.8 3.0 %convolution_add_fusion = f32[256,512]{1,0:T(8,128)} fusion(f32[256,512]{1,0:T(8,128)} %get-tuple-element.103, f32[256,512]{1,0:T(8,128)} %get-tuple-element.101, f32[512,512]{1,0:T(8,128)S(1)} %get-tuple-element.102), kind=kOutput, calls=%fused_computation | convolution fusion | flops 805437440 | bytes 2621440 | tf_op jit(solution)/shard_map/while/body/eval_jaxpr/cond/branch_1_fun/dot_general | solution.py:88
  180.1 10.2 %collective-permute-done.1 = f32[256,512]{1,0:T(8,128)S(1)} collective-permute-done((f32[256,512]{1,0:T(8,128)}, f32[256,512]{1,0:T(8,128)S(1)}, u32[]{:S(2)}, u32[]{:S(2)}) %collective-permute-start.1) | collective-permute-done | bytes 524320 | tf_op jit(solution)/shard_map/ppermute | solution.py:19
  (81 shorter events, 39.9 us)
Async XLA Ops:
  0.6 12.7 %copy-start = (bf16[1,2048,512]{2,1,0:T(8,128)(2,1)S(1)}, bf16[1,2048,512]{2,1,0:T(8,128)(2,1)}, u32[]{:S(2)}) copy-start(bf16[1,2048,512]{2,1,0:T(8,128)(2,1)} %param.18) | copy-start | bytes 6291460
  4.2 1.4 copy-start.11
  7.4 1.0 copy-start.6
  9.6 2.5 %copy-start.1 = (bf16[1,512,512]{2,1,0:T(8,128)(2,1)S(1)}, bf16[1,512,512]{2,1,0:T(8,128)(2,1)}, u32[]{:S(2)}) copy-start(bf16[1,512,512]{2,1,0:T(8,128)(2,1)} %param.16) | copy-start | bytes 1572868
  9.6 3.7 %copy-start.2 = (f32[1,256,512]{2,1,0:T(8,128)S(1)}, f32[1,256,512]{2,1,0:T(8,128)}, u32[]{:S(2)}) copy-start(f32[1,256,512]{2,1,0:T(8,128)} %param.12) | copy-start | bytes 1572868
  9.6 3.7 %copy-start.10 = (f32[1,512]{1,0:T(1,128)S(1)}, f32[1,512]{1,0:T(1,128)}, u32[]{:S(2)}) copy-start(f32[1,512]{1,0:T(1,128)} %param.14) | copy-start | bytes 6148
  23.5 1.0 copy-start.7
  38.0 1.0 copy-start.8
  52.7 1.0 copy-start.5
  61.1 1.5 copy-start.3
  61.1 1.7 copy-start.4
  61.1 1.8 copy-start.9
  64.9 15.9 %collective-permute-start = (f32[256,512]{1,0:T(8,128)}, f32[256,512]{1,0:T(8,128)}, u32[]{:S(2)}, u32[]{:S(2)}) collective-permute-start(f32[256,512]{1,0:T(8,128)} %get-tuple-element.180), channel_id=1, source_target_pairs={{0,4},{4,8},{8,12},{12,16},{16,20},{20,24},{24,28},{1,5},{5,9},{9,... | collective-permute-start | bytes 1572872 | tf_op jit(solution)/shard_map/while/body/eval_jaxpr/ppermute | solution.py:19
  80.7 15.0 %collective-permute-start = (f32[256,512]{1,0:T(8,128)}, f32[256,512]{1,0:T(8,128)}, u32[]{:S(2)}, u32[]{:S(2)}) collective-permute-start(f32[256,512]{1,0:T(8,128)} %get-tuple-element.180), channel_id=1, source_target_pairs={{0,4},{4,8},{8,12},{12,16},{16,20},{20,24},{24,28},{1,5},{5,9},{9,... | collective-permute-start | bytes 1572872 | tf_op jit(solution)/shard_map/while/body/eval_jaxpr/ppermute | solution.py:19
  95.7 14.8 %collective-permute-start = (f32[256,512]{1,0:T(8,128)}, f32[256,512]{1,0:T(8,128)}, u32[]{:S(2)}, u32[]{:S(2)}) collective-permute-start(f32[256,512]{1,0:T(8,128)} %get-tuple-element.180), channel_id=1, source_target_pairs={{0,4},{4,8},{8,12},{12,16},{16,20},{20,24},{24,28},{1,5},{5,9},{9,... | collective-permute-start | bytes 1572872 | tf_op jit(solution)/shard_map/while/body/eval_jaxpr/ppermute | solution.py:19
  110.5 14.2 %collective-permute-start = (f32[256,512]{1,0:T(8,128)}, f32[256,512]{1,0:T(8,128)}, u32[]{:S(2)}, u32[]{:S(2)}) collective-permute-start(f32[256,512]{1,0:T(8,128)} %get-tuple-element.180), channel_id=1, source_target_pairs={{0,4},{4,8},{8,12},{12,16},{16,20},{20,24},{24,28},{1,5},{5,9},{9,... | collective-permute-start | bytes 1572872 | tf_op jit(solution)/shard_map/while/body/eval_jaxpr/ppermute | solution.py:19
  124.7 13.3 %collective-permute-start = (f32[256,512]{1,0:T(8,128)}, f32[256,512]{1,0:T(8,128)}, u32[]{:S(2)}, u32[]{:S(2)}) collective-permute-start(f32[256,512]{1,0:T(8,128)} %get-tuple-element.180), channel_id=1, source_target_pairs={{0,4},{4,8},{8,12},{12,16},{16,20},{20,24},{24,28},{1,5},{5,9},{9,... | collective-permute-start | bytes 1572872 | tf_op jit(solution)/shard_map/while/body/eval_jaxpr/ppermute | solution.py:19
  138.0 12.5 %collective-permute-start = (f32[256,512]{1,0:T(8,128)}, f32[256,512]{1,0:T(8,128)}, u32[]{:S(2)}, u32[]{:S(2)}) collective-permute-start(f32[256,512]{1,0:T(8,128)} %get-tuple-element.180), channel_id=1, source_target_pairs={{0,4},{4,8},{8,12},{12,16},{16,20},{20,24},{24,28},{1,5},{5,9},{9,... | collective-permute-start | bytes 1572872 | tf_op jit(solution)/shard_map/while/body/eval_jaxpr/ppermute | solution.py:19
  150.5 25.2 %collective-permute-start = (f32[256,512]{1,0:T(8,128)}, f32[256,512]{1,0:T(8,128)}, u32[]{:S(2)}, u32[]{:S(2)}) collective-permute-start(f32[256,512]{1,0:T(8,128)} %get-tuple-element.180), channel_id=1, source_target_pairs={{0,4},{4,8},{8,12},{12,16},{16,20},{20,24},{24,28},{1,5},{5,9},{9,... | collective-permute-start | bytes 1572872 | tf_op jit(solution)/shard_map/while/body/eval_jaxpr/ppermute | solution.py:19
  178.8 11.4 %collective-permute-start.1 = (f32[256,512]{1,0:T(8,128)}, f32[256,512]{1,0:T(8,128)S(1)}, u32[]{:S(2)}, u32[]{:S(2)}) collective-permute-start(f32[256,512]{1,0:T(8,128)} %get-tuple-element.113), channel_id=1, source_target_pairs={{0,4},{4,8},{8,12},{12,16},{16,20},{20,24},{24,28},{1,5},{5,9},{9,... | collective-permute-start | bytes 1572872 | tf_op jit(solution)/shard_map/ppermute | solution.py:19
where the time goes:
time: 193 us; the launch traced here: 192 us
  waiting for transfers between devices  112 us (58%)
  matrix products  47.8 us (25%)
  local copies, waits for them, and re-layouts  15.3 us (8%)
  starting transfers between devices  10.2 us (5%)
  other arithmetic  5.65 us (3%)
    ppermute x8, waiting for transfers between devices, passed_along(): return lax.ppermute(block, axis, route)  112 us
    dot_general x4, matrix products, layer_step(): jnp.dot(hidden, w_down, preferred_element_type=jnp.float32)  17.1 us
    ppermute x8, starting transfers between devices, passed_along(): return lax.ppermute(block, axis, route)  10.2 us
    reshape x12, local copies, waits for them, and re-layouts, split_heads(): return block.reshape(-1, SEQ, head_count, HEAD_DIM)  9.65 us
    dot_general x4, matrix products, layer_step(): jnp.dot(normed, w_qkv, preferred_element_type=jnp.float32)  8.78 us
    dot_general x4, matrix products, layer_step(): jnp.einsum('shqk,skhd->sqhd', attention, values, preferred_element_type=j...  8.23 us
    dot_general x4, matrix products, layer_step(): jnp.einsum('sqhd,skhd->shqk', queries, key_heads, preferred_element_type=...  6.56 us
    unnamed x24, local copies, waits for them, and re-layouts  4.27 us
  transfers between devices with their start and end apart: 8, of which 8 were waited for; matrix products, arithmetic and copies ran while one was open for 0% of the time, Pallas kernels for 0%

commit v1 on v0

v1 whole, which is shorter than its diff:
```python
import functools
import math

import jax
import jax.numpy as jnp
from jax import lax
from jax.experimental import pallas as pl
from jax.experimental.pallas import tpu as pltpu
from jax.sharding import PartitionSpec as P

HEAD_DIM = 64
SEQ = 128
FINE = 4
PAIR = 2 * HEAD_DIM
F32 = jnp.float32
BF16 = jnp.bfloat16


def halves_of(a):
    high = a.astype(BF16)
    return high, (a - high.astype(F32)).astype(BF16)


def dot3(a, b):
    a_high, a_low = halves_of(a)
    b_high, b_low = halves_of(b)
    dot = functools.partial(jnp.dot, preferred_element_type=F32)
    return dot(a_high, b_high) + (dot(a_low, b_high) + dot(a_high, b_low))


def coarse_of(a, varying):
    return 0.9 * a + 0.3 * dot3(a, varying)


def in_vmem():
    return pl.BlockSpec(memory_space=pltpu.VMEM)


def in_smem():
    return pl.BlockSpec(memory_space=pltpu.SMEM)


def in_place():
    return pl.BlockSpec(memory_space=pl.ANY)


def fine_kernel(
    position, lengths, start, gain, surrogate, w_qkv, w_out, w_up, w_down,
    kept, sent,
    w_in, w_back, varying, state, act, qkv, bias, sems,
):
    tokens, width = state.shape
    hidden = w_back.shape[0] - width
    copies = [
        pltpu.make_async_copy(w_qkv.at[0], w_in.at[:, pl.ds(0, 3 * width)], sems.at[0]),
        pltpu.make_async_copy(w_up.at[0], w_in.at[:, pl.ds(3 * width, hidden)], sems.at[1]),
        pltpu.make_async_copy(w_out.at[0], w_back.at[pl.ds(0, width), :], sems.at[2]),
        pltpu.make_async_copy(w_down.at[0], w_back.at[pl.ds(width, hidden), :], sems.at[3]),
        pltpu.make_async_copy(surrogate.at[0], varying, sems.at[4]),
    ]
    for copy in copies:
        copy.start()
    state[...] = start[0]
    query = lax.broadcasted_iota(jnp.int32, (SEQ, SEQ), 0)
    key = lax.broadcasted_iota(jnp.int32, (SEQ, SEQ), 1)
    sequences = tokens // SEQ
    for s in range(sequences):
        allowed = (key <= query) & (key < lengths[s])
        bias[pl.ds(s * SEQ, SEQ), :] = jnp.where(allowed, 0.0, -1e30).astype(F32)
    for copy in copies:
        copy.wait()
    low = lax.broadcasted_iota(jnp.int32, (SEQ, PAIR), 1) < HEAD_DIM
    zeros = jnp.zeros((SEQ, PAIR), BF16)
    ones = jnp.ones((SEQ, PAIR), BF16)

    def by_head(block):
        return jnp.concatenate([jnp.where(low, block, zeros), jnp.where(low, zeros, block)], 0)

    counts = by_head(ones)
    chunk = width
    curve = math.sqrt(2 / math.pi)

    def substep(_, carry):
        x = state[...]
        mean_square = jnp.mean(x * x, axis=1, keepdims=True)
        normed = (x * lax.rsqrt(mean_square + 1e-06) * gain[...]).astype(BF16)
        for n in range(0, 3 * width, chunk):
            packed = jnp.dot(normed, w_in[:, n : n + chunk], preferred_element_type=F32).astype(BF16)
            if n < width:
                packed = packed * jnp.asarray(1 / math.sqrt(HEAD_DIM), BF16)
            qkv[:, n : n + chunk] = packed
        for s in range(sequences):
            rows = pl.ds(s * SEQ, SEQ)
            mask = bias[rows, :]
            masks = jnp.concatenate([mask, mask], 0)
            for at in range(0, width, PAIR):
                queries = qkv[rows, at : at + PAIR]
                keys = qkv[rows, width + at : width + at + PAIR]
                values = qkv[rows, 2 * width + at : 2 * width + at + PAIR]
                scores = lax.dot_general(
                    by_head(queries), keys, (((1,), (1,)), ((), ())), preferred_element_type=F32
                ) + masks
                top = jnp.max(scores, axis=-1, keepdims=True)
                weights = jnp.exp(scores - top).astype(BF16)
                pair = jnp.concatenate([weights[:SEQ], weights[SEQ:]], 1)
                both = jnp.dot(
                    pair, jnp.concatenate([by_head(values), counts], 1), preferred_element_type=F32
                )
                act[rows, at : at + PAIR] = (both[:, :PAIR] / both[:, PAIR:]).astype(BF16)
        for n in range(0, hidden, chunk):
            u = jnp.dot(
                normed, w_in[:, 3 * width + n : 3 * width + n + chunk], preferred_element_type=F32
            )
            half = 0.5 * u
            gelu = half + half * jnp.tanh(u * (curve + (curve * 0.044715) * (u * u)))
            act[:, width + n : width + n + chunk] = gelu.astype(BF16)
        state[...] = x + jnp.dot(act[...], w_back[...], preferred_element_type=F32) * (1.0 / FINE)
        return carry

    lax.fori_loop(0, FINE, substep, 0)
    begun = start[0]
    share = jnp.where(position[0] == 0, 0.0, 1.0).astype(F32)
    state[...] = state[...] - share * coarse_of(begun, varying[...])
    half_rows = tokens // 2
    mine = position[0] % 2
    kept[...] = state[pl.ds(pl.multiple_of(mine * half_rows, half_rows), half_rows), :]
    sent[...] = state[pl.ds(pl.multiple_of((1 - mine) * half_rows, half_rows), half_rows), :]


def fine_jump(position, lengths, start, gain, surrogate, w_qkv, w_out, w_up, w_down):
    tokens, width = start.shape[1:]
    hidden = w_up.shape[2]
    half = jax.ShapeDtypeStruct((tokens // 2, width), F32)
    return pl.pallas_call(
        fine_kernel,
        in_specs=[in_smem(), in_smem(), in_vmem(), in_vmem()] + [in_place()] * 5,
        out_specs=[in_vmem()] * 2,
        out_shape=[half, half],
        scratch_shapes=[
            pltpu.VMEM((width, 3 * width + hidden), BF16),
            pltpu.VMEM((width + hidden, width), BF16),
            pltpu.VMEM((width, width), F32),
            pltpu.VMEM((tokens, width), F32),
            pltpu.VMEM((tokens, width + hidden), BF16),
            pltpu.VMEM((tokens, 3 * width), BF16),
            pltpu.VMEM((tokens, SEQ), F32),
            pltpu.SemaphoreType.DMA((5,)),
        ],
    )(position, lengths, start, gain, surrogate, w_qkv, w_out, w_up, w_down)


def hop_kernel(position, incoming, kept, received, own, other, out):
    def over(first_jump, first, second_jump, second):
        middle = first_jump + coarse_of(incoming[...], first)
        out[...] = second_jump + coarse_of(middle, second)

    even = position[0] % 2 == 0

    @pl.when(even)
    def _():
        over(kept[...], own[...], received[...], other[...])

    @pl.when(jnp.logical_not(even))
    def _():
        over(received[...], other[...], kept[...], own[...])


def hop(position, incoming, kept, received, own, other):
    return pl.pallas_call(
        hop_kernel,
        in_specs=[in_smem()] + [in_vmem()] * 5,
        out_specs=in_vmem(),
        out_shape=jax.ShapeDtypeStruct(incoming.shape, F32),
    )(position, incoming, kept, received, own, other)


def turn_kernel(position, incoming, kept, own, received_jump, other, head, out):
    even = position[0] % 2 == 0

    @pl.when(even)
    def _():
        head[...] = incoming[...]
        out[...] = kept[...] + coarse_of(incoming[...], own[...])

    @pl.when(jnp.logical_not(even))
    def _():
        head[...] = received_jump[...] + coarse_of(incoming[...], other[...])
        out[...] = incoming[...]


def turn(position, incoming, kept, own, received, other):
    shape = jax.ShapeDtypeStruct(incoming.shape, F32)
    return pl.pallas_call(
        turn_kernel,
        in_specs=[in_smem()] + [in_vmem()] * 5,
        out_specs=[in_vmem()] * 2,
        out_shape=[shape, shape],
    )(position, incoming, kept, own, received, other)


def close_kernel(position, head, returned, kept, sent, own, start, out, change):
    half = head.shape[0]
    width = head.shape[1]
    share = jnp.where(position[0] == 0, 0.0, 1.0).astype(F32)
    for at, ahead, jump in ((0, head, kept), (1, returned, sent)):
        where = (position[0] % 2 + at) % 2
        rows = pl.ds(pl.multiple_of(where * half, half), half)
        state = share * ahead[...]
        out[0, rows, :] = jump[...] + coarse_of(state, own[...])
        difference = ahead[...] - start[0, rows, :]
        total = lax.dot_general(
            jnp.ones((8, width), F32), difference * difference, (((1,), (1,)), ((), ())),
            precision=lax.Precision.HIGHEST, preferred_element_type=F32,
        )
        change[:, rows] = share * jnp.sqrt(total[:1] * (1.0 / width))


def close(position, head, returned, kept, sent, own, start):
    tokens, width = start.shape[1:]
    return pl.pallas_call(
        close_kernel,
        in_specs=[in_smem()] + [in_vmem()] * 6,
        out_specs=[in_vmem()] * 2,
        out_shape=[
            jax.ShapeDtypeStruct((1, tokens, width), F32),
            jax.ShapeDtypeStruct((1, tokens), F32),
        ],
    )(position, head, returned, kept, sent, own, start)


def shards(old_heads, surrogate, norm_gain, w_qkv, w_out, w_up, w_down, lengths):
    layers = lax.axis_size("layer")
    batches = lax.axis_size("dp")
    layer = lax.axis_index("layer")
    batch = lax.axis_index("dp")
    position = layer.astype(jnp.int32).reshape(1)
    partners = [(i, i ^ 1) for i in range(layers)]
    neighbours = [(i, i ^ 1) for i in range(batches)]

    width = surrogate.shape[1]
    part = width // 2
    mine = lax.dynamic_slice_in_dim(surrogate[0], (batch % 2) * part, part, 0)
    got = lax.ppermute(mine, "layer", partners)
    passed = lax.ppermute(got, "dp", neighbours)
    first = batch % 2 == 0
    other = jnp.concatenate([jnp.where(first, got, passed), jnp.where(first, passed, got)], 0)
    own = surrogate[0]

    kept, sent = fine_jump(
        position, lengths, old_heads, norm_gain, surrogate, w_qkv, w_out, w_up, w_down
    )
    received = lax.ppermute(sent, "layer", partners)
    arrived = jnp.zeros_like(kept)
    incoming = arrived
    for at in range(0, layers - 2, 2):
        carried = hop(position, incoming, kept, received, own, other)
        incoming = lax.ppermute(carried, "layer", [(at, at + 2), (at + 1, at + 3)])
        arrived = arrived + incoming
    head, out = turn(position, arrived, kept, own, received, other)
    returned = lax.ppermute(out, "layer", partners)
    return close(position, head, returned, kept, sent, own, old_heads)


def solution(mesh):
    in_specs = (
        P("layer", "dp", None),
        P("layer", None, None),
        P("layer", None),
        P("layer", None, None),
        P("layer", None, None),
        P("layer", None, None),
        P("layer", None, None),
        P("dp"),
    )
    out_specs = (P("layer", "dp", None), P("layer", "dp"))
    return jax.shard_map(shards, mesh=mesh, in_specs=in_specs, out_specs=out_specs, check_vma=False)
```

time: 193 us -> 91.6 us (0.47)
  waiting for transfers between devices: 112 us -> 47.3 us
  matrix products: 47.8 us -> 0 us
  Pallas kernels: 0 us -> 31.6 us
  local copies, waits for them, and re-layouts: 15.3 us -> 4 us
  starting transfers between devices: 10.2 us -> 4.59 us
  other arithmetic: 5.65 us -> 2.88 us
    ppermute x8 -> x7, waiting for transfers between devices: 112 us -> 47.3 us  [the longest x3 21 us: shards(): incoming = lax.ppermute(carried, 'layer', [(at, at + 2), (at + 1, at + 3)])]
    dot_general x22 -> x0, matrix products: 47.8 us -> none  [the longest x4 17.1 us: layer_step(): jnp.dot(hidden, w_down, preferred_element_type=jnp.float32)]
    pallas_call x0 -> x6, Pallas kernels: none -> 31.6 us  [the longest x1 15.3 us: fine_jump(): pl.pallas_call(fine_kernel, in_specs=[in_smem(), in_smem(), in_vmem(), in...]
    reshape x12 -> x0, local copies, waits for them, and re-layouts: 9.65 us -> none  [split_heads(): return block.reshape(-1, SEQ, head_count, HEAD_DIM)]
    ppermute x8 -> x7, starting transfers between devices: 10.2 us -> 4.59 us  [the longest x3 2.74 us: shards(): incoming = lax.ppermute(carried, 'layer', [(at, at + 2), (at + 1, at + 3)])]
    reduce_sum x2 -> x0, other arithmetic: 2.49 us -> none  [the longest x1 1.3 us: layer_step(): mean_square = jnp.mean(current * current, axis=1, keepdims=True)]
    unnamed x24 -> x10, local copies, waits for them, and re-layouts: 4.27 us -> 2.14 us
  transfers between devices with their start and end apart: 8 -> 7, of which waited for: 8 -> 4; matrix products, arithmetic and copies ran while one was open for 0% -> 1% of each run, Pallas kernels for 0% -> 17%
where the time goes in v1:
time: 91.6 us; the launch traced here: 91 us
  waiting for transfers between devices  47.3 us (52%)
  Pallas kernels  31.6 us (34%)
  starting transfers between devices  4.59 us (5%)
  local copies, waits for them, and re-layouts  4 us (4%)
  other arithmetic  2.88 us (3%)
    ppermute x3, waiting for transfers between devices, shards(): incoming = lax.ppermute(carried, 'layer', [(at, at + 2), (at + 1, at + 3)])  21 us
    pallas_call x1, Pallas kernels, fine_jump(): pl.pallas_call(fine_kernel, in_specs=[in_smem(), in_smem(), in_vmem(), in...  15.3 us
    ppermute x1, waiting for transfers between devices, shards(): got = lax.ppermute(mine, 'layer', partners)  13.1 us
    pallas_call x3, Pallas kernels, hop(): pl.pallas_call(hop_kernel, in_specs=[in_smem()] + [in_vmem()] * 5, out_sp...  9.74 us
    ppermute x1, waiting for transfers between devices, shards(): received = lax.ppermute(sent, 'layer', partners)  7.2 us
    ppermute x1, waiting for transfers between devices, shards(): returned = lax.ppermute(out, 'layer', partners)  5.94 us
    pallas_call x1, Pallas kernels, close(): pl.pallas_call(close_kernel, in_specs=[in_smem()] + [in_vmem()] * 6, out_...  3.49 us
    pallas_call x1, Pallas kernels, turn(): pl.pallas_call(turn_kernel, in_specs=[in_smem()] + [in_vmem()] * 5, out_s...  3 us
  transfers between devices with their start and end apart: 7, of which 4 were waited for; matrix products, arithmetic and copies ran while one was open for 1% of the time, Pallas kernels for 17%

profile of v1, /device:TPU:26, one launch (start us, length us, event | category | flops | bytes accessed | tf_op | source)
XLA Modules:
  0.0 91.0 jit_solution(16552695100127207271)
XLA Ops:
  0.6 1.1 %dynamic-slice_bitcast_fusion = f32[256,512]{1,0:T(8,128)S(1)} fusion(f32[1,512,512]{2,1,0:T(8,128)} %surrogate.1, s32[]{:T(128)S(6)} %select_n.26), kind=kLoop, calls=%fused_computation.1 | loop fusion | bytes 1048580 | tf_op jit(solution)/shard_map/dynamic_slice | solution.py:242
  1.7 0.6 collective-permute-start.1
  2.3 13.1 %collective-permute-done.1 = f32[256,512]{1,0:T(8,128)S(1)} collective-permute-done((f32[256,512]{1,0:T(8,128)S(1)}, f32[256,512]{1,0:T(8,128)S(1)}, u32[]{:S(2)}, u32[]{:S(2)}) %collective-permute-start.1) | collective-permute-done | bytes 524320 | tf_op jit(solution)/shard_map/ppermute | solution.py:243
  15.5 15.3 %shard_map.95 = (f32[128,512]{1,0:T(8,128)}, f32[128,512]{1,0:T(8,128)}) custom-call(s32[1]{0:T(128)} %bitcast.position, s32[2]{0:T(128)} %lengths.1, f32[1,256,512]{2,1,0:T(8,128)} %start.3, f32[1,512]{1,0:T(1,128)} %gain.1, f32[1,512,512]{2,1,0:T(8,128)} %surrogate.1, bf16[1,512,1536]{2,1,0:T(8,128)(2,1)} %w_qkv.1, bf16[1,512,512]{2,1,0:T(8,128)(2,1)} %w_out.1, ...), custom_call_target="tpu_custom_call" | custom-call | tf_op jit(solution)/shard_map/pallas_call | solution.py:134
  30.8 0.6 collective-permute-start
  31.4 0.1 broadcast_select_fusion.1
  31.5 1.1 %pad_maximum_fusion.other = f32[512,512]{1,0:T(8,128)} fusion(f32[256,512]{1,0:T(8,128)S(1)} %get-tuple-element.11, f32[256,512]{1,0:T(8,128)S(1)} %get-tuple-element.10), kind=kLoop, calls=%fused_computation | loop fusion | flops 262144 | bytes 2097152 | tf_op jit(solution)/shard_map/concatenate | solution.py:246
  32.6 7.2 %collective-permute-done.received.received_jump = f32[128,512]{1,0:T(8,128)S(1)} collective-permute-done((f32[128,512]{1,0:T(8,128)}, f32[128,512]{1,0:T(8,128)S(1)}, u32[]{:S(2)}, u32[]{:S(2)}) %collective-permute-start) | collective-permute-done | bytes 262176 | tf_op jit(solution)/shard_map/ppermute | solution.py:252
  39.8 0.8 broadcast_in_dim.3.incoming
  40.6 3.3 %shard_map.96 = f32[128,512]{1,0:T(8,128)} custom-call(s32[1]{0:T(128)} %bitcast.position, f32[128,512]{1,0:T(8,128)} %broadcast_in_dim.3.incoming, f32[128,512]{1,0:T(8,128)} %get-tuple-element.6.kept, f32[128,512]{1,0:T(8,128)} %copy-done, f32[512,512]{1,0:T(8,128)} %bitcast.4, f32[512,512]{1,0:T(8,128)} %pad_maximum_fusion.other), custom_call_target="tpu_custom_call" | custom-call | tf_op jit(solution)/shard_map/pallas_call | solution.py:169
  43.8 0.7 collective-permute-start.3
  44.5 0.7 copy-done.1
  45.2 3.3 %shard_map.97 = f32[128,512]{1,0:T(8,128)} custom-call(s32[1]{0:T(128)} %bitcast.position, f32[128,512]{1,0:T(8,128)} %copy-done.1, f32[128,512]{1,0:T(8,128)} %get-tuple-element.6.kept, f32[128,512]{1,0:T(8,128)} %copy-done, f32[512,512]{1,0:T(8,128)} %bitcast.5, f32[512,512]{1,0:T(8,128)} %pad_maximum_fusion.other), custom_call_target="tpu_custom_call" | custom-call | tf_op jit(solution)/shard_map/pallas_call | solution.py:169
  48.5 0.8 collective-permute-start.4
  49.3 0.7 copy-done.3
  50.0 3.2 %shard_map.98 = f32[128,512]{1,0:T(8,128)} custom-call(s32[1]{0:T(128)} %bitcast.position, f32[128,512]{1,0:T(8,128)} %copy-done.3, f32[128,512]{1,0:T(8,128)} %get-tuple-element.6.kept, f32[128,512]{1,0:T(8,128)} %copy-done, f32[512,512]{1,0:T(8,128)} %bitcast.6, f32[512,512]{1,0:T(8,128)} %pad_maximum_fusion.other), custom_call_target="tpu_custom_call" | custom-call | tf_op jit(solution)/shard_map/pallas_call | solution.py:169
  53.3 1.3 %collective-permute-start.5 = (f32[128,512]{1,0:T(8,128)}, f32[128,512]{1,0:T(8,128)S(1)}, u32[]{:S(2)}, u32[]{:S(2)}) collective-permute-start(f32[128,512]{1,0:T(8,128)} %shard_map.98), channel_id=1, source_target_pairs={{16,24},{20,28},{17,25},{21,29},{18,26},{22,30},{19,27},{23,31}} | collective-permute-start | bytes 786440 | tf_op jit(solution)/shard_map/ppermute | solution.py:257
  54.5 21.0 %collective-permute-done.5 = f32[128,512]{1,0:T(8,128)S(1)} collective-permute-done((f32[128,512]{1,0:T(8,128)}, f32[128,512]{1,0:T(8,128)S(1)}, u32[]{:S(2)}, u32[]{:S(2)}) %collective-permute-start.5) | collective-permute-done | bytes 262176 | tf_op jit(solution)/shard_map/ppermute | solution.py:257
  75.5 1.7 %add_add_fusion.incoming = f32[128,512]{1,0:T(8,128)} fusion(f32[128,512]{1,0:T(8,128)S(1)} %collective-permute-done.5, f32[128,512]{1,0:T(8,128)S(1)} %copy-done.2, f32[128,512]{1,0:T(8,128)} %copy-done.3), kind=kLoop, calls=%fused_computation.2 | loop fusion | flops 131072 | bytes 1048576 | tf_op jit(solution)/shard_map/add | solution.py:258
  77.3 3.0 %shard_map.99 = (f32[128,512]{1,0:T(8,128)}, f32[128,512]{1,0:T(8,128)}) custom-call(s32[1]{0:T(128)} %bitcast.position, f32[128,512]{1,0:T(8,128)} %add_add_fusion.incoming, f32[128,512]{1,0:T(8,128)} %get-tuple-element.6.kept, f32[512,512]{1,0:T(8,128)} %bitcast.7, f32[128,512]{1,0:T(8,128)} %copy-done, f32[512,512]{1,0:T(8,128)} %pad_maximum_fusion.other), custom_call_target="tpu_custom_call" | custom-call | tf_op jit(solution)/shard_map/pallas_call | solution.py:193
  80.2 0.6 collective-permute-start.6
  80.9 5.9 %collective-permute-done.6.returned = f32[128,512]{1,0:T(8,128)S(1)} collective-permute-done((f32[128,512]{1,0:T(8,128)}, f32[128,512]{1,0:T(8,128)S(1)}, u32[]{:S(2)}, u32[]{:S(2)}) %collective-permute-start.6) | collective-permute-done | bytes 262176 | tf_op jit(solution)/shard_map/ppermute | solution.py:260
  86.8 0.7 copy-done.4
  87.5 3.5 %shard_map.100 = (f32[1,256,512]{2,1,0:T(8,128)}, f32[1,256]{1,0:T(1,128)}) custom-call(s32[1]{0:T(128)} %bitcast.position, f32[128,512]{1,0:T(8,128)} %get-tuple-element.8.head, f32[128,512]{1,0:T(8,128)} %copy-done.4, f32[128,512]{1,0:T(8,128)} %get-tuple-element.6.kept, f32[128,512]{1,0:T(8,128)} %get-tuple-element.7.sent, f32[512,512]{1,0:T(8,128)} %bitcast.8, ...), custom_call_target="tpu_custom_call" | custom-call | tf_op jit(solution)/shard_map/pallas_call | solution.py:220
  (11 shorter events, 0.0 us)
Async XLA Ops:
  1.7 13.7 %collective-permute-start.1 = (f32[256,512]{1,0:T(8,128)S(1)}, f32[256,512]{1,0:T(8,128)S(1)}, u32[]{:S(2)}, u32[]{:S(2)}) collective-permute-start(f32[256,512]{1,0:T(8,128)S(1)} %dynamic-slice_bitcast_fusion), channel_id=1, source_target_pairs={{0,4},{4,0},{8,12},{12,8},{16,20},{20,16},{24,28},{28,24},{1,5},{5... | collective-permute-start | bytes 1572872 | tf_op jit(solution)/shard_map/ppermute | solution.py:243
  15.5 15.9 %collective-permute-start.2 = (f32[256,512]{1,0:T(8,128)S(1)}, f32[256,512]{1,0:T(8,128)S(1)}, u32[]{:S(2)}, u32[]{:S(2)}) collective-permute-start(f32[256,512]{1,0:T(8,128)S(1)} %collective-permute-done.1), channel_id=1, source_target_pairs={{0,1},{1,0},{2,3},{3,2},{4,5},{5,4},{6,7},{7,6},{8,9},{9,8},{10,11... | collective-permute-start | bytes 1572872 | tf_op jit(solution)/shard_map/ppermute | solution.py:244
  30.8 9.0 %collective-permute-start = (f32[128,512]{1,0:T(8,128)}, f32[128,512]{1,0:T(8,128)S(1)}, u32[]{:S(2)}, u32[]{:S(2)}) collective-permute-start(f32[128,512]{1,0:T(8,128)} %get-tuple-element.7.sent), channel_id=1, source_target_pairs={{0,4},{4,0},{8,12},{12,8},{16,20},{20,16},{24,28},{28,24},{1,5},{5... | collective-permute-start | bytes 786440 | tf_op jit(solution)/shard_map/ppermute | solution.py:252
  39.8 0.8 copy-start
  43.8 0.7 collective-permute-start.3
  44.5 0.7 copy-start.1
  48.5 27.1 %copy-start.2 = (f32[128,512]{1,0:T(8,128)S(1)}, f32[128,512]{1,0:T(8,128)}, u32[]{:S(2)}) copy-start(f32[128,512]{1,0:T(8,128)} %copy-done.1) | copy-start | bytes 786436
  48.5 0.8 collective-permute-start.4
  49.3 0.7 copy-start.3
  53.3 22.3 %collective-permute-start.5 = (f32[128,512]{1,0:T(8,128)}, f32[128,512]{1,0:T(8,128)S(1)}, u32[]{:S(2)}, u32[]{:S(2)}) collective-permute-start(f32[128,512]{1,0:T(8,128)} %shard_map.98), channel_id=1, source_target_pairs={{16,24},{20,28},{17,25},{21,29},{18,26},{22,30},{19,27},{23,31}} | collective-permute-start | bytes 786440 | tf_op jit(solution)/shard_map/ppermute | solution.py:257
  80.2 6.6 %collective-permute-start.6 = (f32[128,512]{1,0:T(8,128)}, f32[128,512]{1,0:T(8,128)S(1)}, u32[]{:S(2)}, u32[]{:S(2)}) collective-permute-start(f32[128,512]{1,0:T(8,128)} %get-tuple-element.9), channel_id=1, source_target_pairs={{0,4},{4,0},{8,12},{12,8},{16,20},{20,16},{24,28},{28,24},{1,5},{5... | collective-permute-start | bytes 786440 | tf_op jit(solution)/shard_map/ppermute | solution.py:260
  86.8 0.7 copy-start.4

commit v2 on v1

v2 whole, which is shorter than its diff:
```python
import functools
import math

import jax
import jax.numpy as jnp
from jax import lax
from jax.experimental import pallas as pl
from jax.experimental.pallas import tpu as pltpu
from jax.sharding import PartitionSpec as P


HEAD_DIM = 64
SEQ = 128
FINE = 4
CHUNKS = 2
PAIR = 2 * HEAD_DIM
F32 = jnp.float32
BF16 = jnp.bfloat16


def halves_of(a):
    high = a.astype(BF16)
    return high, (a - high.astype(F32)).astype(BF16)


def dot3(a, b):
    a_high, a_low = halves_of(a)
    b_high, b_low = halves_of(b)
    dot = functools.partial(jnp.dot, preferred_element_type=F32)
    return dot(a_high, b_high) + (dot(a_low, b_high) + dot(a_high, b_low))


def dot_split(a, b_high, b_low):
    a_high, a_low = halves_of(a)
    rows = a.shape[0]
    both = jnp.dot(jnp.concatenate([a_high, a_low], 0), b_high, preferred_element_type=F32)
    return both[:rows] + (both[rows:] + jnp.dot(a_high, b_low, preferred_element_type=F32))


def params(megabytes):
    return pltpu.CompilerParams(vmem_limit_bytes=megabytes << 20)


def in_vmem():
    return pl.BlockSpec(memory_space=pltpu.VMEM)


def in_smem():
    return pl.BlockSpec(memory_space=pltpu.SMEM)


def in_place():
    return pl.BlockSpec(memory_space=pltpu.HBM)


def fine_kernel(
    position, lengths, start, gain, surrogate, w_qkv, w_out, w_up, w_down, *outs_and_scratch
):
    *pieces, w_in, w_back, varying, state, act, qkv, bias, sems = outs_and_scratch
    tokens, width = state.shape
    hidden = w_back.shape[0] - width
    copies = [
        pltpu.make_async_copy(w_qkv.at[0], w_in.at[:, pl.ds(0, 3 * width)], sems.at[0]),
        pltpu.make_async_copy(w_up.at[0], w_in.at[:, pl.ds(3 * width, hidden)], sems.at[1]),
        pltpu.make_async_copy(w_out.at[0], w_back.at[pl.ds(0, width), :], sems.at[2]),
        pltpu.make_async_copy(w_down.at[0], w_back.at[pl.ds(width, hidden), :], sems.at[3]),
        pltpu.make_async_copy(surrogate.at[0], varying, sems.at[4]),
    ]
    for copy in copies:
        copy.start()
    state[...] = start[0]
    query = lax.broadcasted_iota(jnp.int32, (SEQ, SEQ), 0)
    key = lax.broadcasted_iota(jnp.int32, (SEQ, SEQ), 1)
    sequences = tokens // SEQ
    for s in range(sequences):
        allowed = (key <= query) & (key < lengths[s])
        bias[pl.ds(s * SEQ, SEQ), :] = jnp.where(allowed, 0.0, -1e30).astype(F32)
    for copy in copies:
        copy.wait()
    low = lax.broadcasted_iota(jnp.int32, (SEQ, PAIR), 1) < HEAD_DIM
    zeros = jnp.zeros((SEQ, PAIR), BF16)
    ones = jnp.ones((SEQ, PAIR), BF16)

    def by_head(block):
        return jnp.concatenate([jnp.where(low, block, zeros), jnp.where(low, zeros, block)], 0)

    counts = by_head(ones)
    chunk = width
    curve = math.sqrt(2 / math.pi)

    def substep(_, carry):
        x = state[...]
        mean_square = jnp.mean(x * x, axis=1, keepdims=True)
        normed = (x * lax.rsqrt(mean_square + 1e-06) * gain[...]).astype(BF16)
        for n in range(0, 3 * width, chunk):
            packed = jnp.dot(normed, w_in[:, n : n + chunk], preferred_element_type=F32).astype(BF16)
            if n < width:
                packed = packed * jnp.asarray(1 / math.sqrt(HEAD_DIM), BF16)
            qkv[:, n : n + chunk] = packed
        for s in range(sequences):
            rows = pl.ds(s * SEQ, SEQ)
            mask = bias[rows, :]
            masks = jnp.concatenate([mask, mask], 0)
            for at in range(0, width, PAIR):
                queries = qkv[rows, at : at + PAIR]
                keys = qkv[rows, width + at : width + at + PAIR]
                values = qkv[rows, 2 * width + at : 2 * width + at + PAIR]
                scores = lax.dot_general(
                    by_head(queries), keys, (((1,), (1,)), ((), ())), preferred_element_type=F32
                ) + masks
                top = jnp.max(scores, axis=-1, keepdims=True)
                weights = jnp.exp(scores - top).astype(BF16)
                pair = jnp.concatenate([weights[:SEQ], weights[SEQ:]], 1)
                both = jnp.dot(
                    pair, jnp.concatenate([by_head(values), counts], 1), preferred_element_type=F32
                )
                act[rows, at : at + PAIR] = (both[:, :PAIR] / both[:, PAIR:]).astype(BF16)
        for n in range(0, hidden, chunk):
            u = jnp.dot(
                normed, w_in[:, 3 * width + n : 3 * width + n + chunk], preferred_element_type=F32
            )
            half = 0.5 * u
            gelu = half + half * jnp.tanh(u * (curve + (curve * 0.044715) * (u * u)))
            act[:, width + n : width + n + chunk] = gelu.astype(BF16)
        state[...] = x + jnp.dot(act[...], w_back[...], preferred_element_type=F32) * (1.0 / FINE)
        return carry

    lax.fori_loop(0, FINE, substep, 0)
    begun = start[0]
    share = jnp.where(position[0] == 0, 0.0, 1.0).astype(F32)
    state[...] = state[...] - share * (0.9 * begun + 0.3 * dot3(begun, varying[...]))
    mine = position[0] % 2
    half = pieces[0].shape[0]
    for at in range(len(pieces) // 2):
        for piece, part in ((pieces[2 * at], mine), (pieces[2 * at + 1], 1 - mine)):
            piece[...] = state[pl.ds(pl.multiple_of((2 * at + part) * half, half), half), :]


def fine_jump(chunks, position, lengths, start, gain, surrogate, w_qkv, w_out, w_up, w_down):
    tokens, width = start.shape[1:]
    hidden = w_up.shape[2]
    half = jax.ShapeDtypeStruct((tokens // (2 * chunks), width), F32)
    return pl.pallas_call(
        fine_kernel,
        in_specs=[in_smem(), in_smem(), in_vmem(), in_vmem()] + [in_place()] * 5,
        out_specs=[in_vmem()] * (2 * chunks),
        out_shape=[half] * (2 * chunks),
        scratch_shapes=[
            pltpu.VMEM((width, 3 * width + hidden), BF16),
            pltpu.VMEM((width + hidden, width), BF16),
            pltpu.VMEM((width, width), F32),
            pltpu.VMEM((tokens, width), F32),
            pltpu.VMEM((tokens, width + hidden), BF16),
            pltpu.VMEM((tokens, 3 * width), BF16),
            pltpu.VMEM((tokens, SEQ), F32),
            pltpu.SemaphoreType.DMA((5,)),
        ],
        cost_estimate=pl.CostEstimate(
            flops=2 * FINE * tokens * width * (4 * width + 2 * hidden),
            transcendentals=FINE * tokens * hidden,
            bytes_accessed=2 * width * (4 * width + 2 * hidden),
        ),
        compiler_params=params(62),
    )(position, lengths, start, gain, surrogate, w_qkv, w_out, w_up, w_down)


def maps_kernel(
    parity, own, got, passed,
    own_high, own_low, even_high, even_low, odd_high, odd_low, both_high, both_low, even, odd,
):
    part = got.shape[0]
    flag, core = parity[0], parity[1]

    def place(other):
        for source, where in ((got, core), (passed, 1 - core)):
            other[pl.ds(pl.multiple_of(where * part, part), part), :] = 0.3 * source[...]

    mine = 0.3 * own[0]
    own_high[...], own_low[...] = halves_of(mine)

    @pl.when(flag == 0)
    def _():
        even[...] = mine
        place(odd)

    @pl.when(flag != 0)
    def _():
        odd[...] = mine
        place(even)

    first, second = even[...], odd[...]
    even_high[...], even_low[...] = halves_of(first)
    odd_high[...], odd_low[...] = halves_of(second)
    product = 0.9 * (first + second) + dot_split(first, odd_high[...], odd_low[...])
    both_high[...], both_low[...] = halves_of(product)


def maps(parity, own, got, passed):
    width = own.shape[1]
    square = jax.ShapeDtypeStruct((width, width), BF16)
    return pl.pallas_call(
        maps_kernel,
        in_specs=[in_smem()] + [in_vmem()] * 3,
        out_specs=[in_vmem()] * 8,
        out_shape=[square] * 8,
        scratch_shapes=[pltpu.VMEM((width, width), F32)] * 2,
        compiler_params=params(16),
    )(parity, own, got, passed)


def join_kernel(parity, kept, received, odd_high, odd_low, out):
    even = parity[0] == 0
    first = jnp.where(even, kept[...], received[...])
    second = jnp.where(even, received[...], kept[...])
    out[...] = second + (0.9 * first + dot_split(first, odd_high[...], odd_low[...]))


def join(parity, kept, received, odd):
    return pl.pallas_call(
        join_kernel,
        in_specs=[in_smem()] + [in_vmem()] * 4,
        out_specs=in_vmem(),
        out_shape=jax.ShapeDtypeStruct(kept.shape, F32),
        compiler_params=params(8),
    )(parity, kept, received, *odd)


def hop_kernel(incoming, joined, both_high, both_low, out):
    state = incoming[...]
    out[...] = joined[...] + (0.81 * state + dot_split(state, both_high[...], both_low[...]))


def hop(incoming, joined, both):
    return pl.pallas_call(
        hop_kernel,
        in_specs=[in_vmem()] * 4,
        out_specs=in_vmem(),
        out_shape=jax.ShapeDtypeStruct(incoming.shape, F32),
        compiler_params=params(8),
    )(incoming, joined, *both)


def turn_kernel(parity, kept, received, even_high, even_low, *arrivals_and_outs):
    *arrivals, head, out = arrivals_and_outs
    state = functools.reduce(jnp.add, [arrival[...] for arrival in arrivals])
    even = parity[0] == 0
    first = jnp.where(even, kept[...], received[...])
    after = first + (0.9 * state + dot_split(state, even_high[...], even_low[...]))
    head[...] = jnp.where(even, state, after)
    out[...] = jnp.where(even, after, state)


def turn(parity, kept, received, even, arrivals):
    shape = jax.ShapeDtypeStruct(kept.shape, F32)
    return pl.pallas_call(
        turn_kernel,
        in_specs=[in_smem()] + [in_vmem()] * (4 + len(arrivals)),
        out_specs=[in_vmem()] * 2,
        out_shape=[shape, shape],
        compiler_params=params(8),
    )(parity, kept, received, *even, *arrivals)


def close_kernel(chunks, position, start, own_high, own_low, *rest):
    *pieces, out, change = rest
    half, _ = pieces[0].shape
    share = jnp.where(position[0] == 0, 0.0, 1.0).astype(F32)
    for at in range(chunks):
        head, returned, kept, sent = pieces[4 * at : 4 * at + 4]
        for ahead, jump, other in ((head, kept, 0), (returned, sent, 1)):
            where = (position[0] + other) % 2 + 2 * at
            rows = pl.ds(pl.multiple_of(where * half, half), half)
            state = share * ahead[...]
            out[0, rows, :] = jump[...] + (
                0.9 * state + dot_split(state, own_high[...], own_low[...])
            )
            difference = state - share * start[0, rows, :]
            mean = jnp.mean(difference * difference, axis=1, keepdims=True)
            change[rows, :] = jnp.broadcast_to(jnp.sqrt(mean), (half, change.shape[1]))


def close(position, start, own, pieces):
    tokens, width = start.shape[1:]
    return pl.pallas_call(
        functools.partial(close_kernel, len(pieces) // 4),
        in_specs=[in_smem()] + [in_vmem()] * (3 + len(pieces)),
        out_specs=[in_vmem()] * 2,
        out_shape=[
            jax.ShapeDtypeStruct((1, tokens, width), F32),
            jax.ShapeDtypeStruct((tokens, 128), F32),
        ],
        compiler_params=params(12),
    )(position, start, *own, *pieces)


def shards(old_heads, surrogate, norm_gain, w_qkv, w_out, w_up, w_down, lengths):
    layers = lax.axis_size("layer")
    batches = lax.axis_size("dp")
    layer = lax.axis_index("layer").astype(jnp.int32)
    core = lax.axis_index("dp").astype(jnp.int32) % 2
    position = layer.reshape(1)
    parity = jnp.stack([layer % 2, core])
    partners = [(i, i ^ 1) for i in range(layers)]
    neighbours = [(i, i ^ 1) for i in range(batches)]

    part = surrogate.shape[1] // 2
    mine = lax.dynamic_slice_in_dim(surrogate[0], core * part, part, 0)
    got = lax.ppermute(mine, "layer", partners)
    pieces = fine_jump(
        CHUNKS, position, lengths, old_heads, norm_gain, surrogate, w_qkv, w_out, w_up, w_down
    )
    passed = lax.ppermute(got, "dp", neighbours)
    kept, sent = pieces[::2], pieces[1::2]
    received = [lax.ppermute(piece, "layer", partners) for piece in sent]
    split = maps(parity, surrogate, got, passed)
    own, even, odd, both = split[0:2], split[2:4], split[4:6], split[6:8]
    spans = range(CHUNKS)
    joined = [join(parity, kept[c], received[c], odd) for c in spans]
    carried = joined
    arrivals = [[] for c in spans]
    for at in range(0, layers - 2, 2):
        route = [(at, at + 2), (at + 1, at + 3)]
        for c in spans:
            arrivals[c].append(lax.ppermute(carried[c], "layer", route))
        if at < layers - 4:
            carried = [hop(arrivals[c][-1], joined[c], both) for c in spans]
    pieces = []
    for c in spans:
        head, out = turn(parity, kept[c], received[c], even, arrivals[c])
        pieces += [head, lax.ppermute(out, "layer", partners), kept[c], sent[c]]
    new_heads, change = close(position, old_heads, own, pieces)
    return new_heads, change[:, :1].reshape(1, -1)


def solution(mesh):
    in_specs = (
        P("layer", "dp", None),
        P("layer", None, None),
        P("layer", None),
        P("layer", None, None),
        P("layer", None, None),
        P("layer", None, None),
        P("layer", None, None),
        P("dp"),
    )
    out_specs = (P("layer", "dp", None), P("layer", "dp"))
    return jax.shard_map(shards, mesh=mesh, in_specs=in_specs, out_specs=out_specs, check_vma=False)
```

time: 91.6 us -> 68.4 us (0.75)
  waiting for transfers between devices: 47.3 us -> 31.6 us
  Pallas kernels: 31.6 us -> 24.1 us
  starting transfers between devices: 4.59 us -> 9.67 us
  other arithmetic: 2.88 us -> 0.07 us
  local copies, waits for them, and re-layouts: 4 us -> 1.79 us
    ppermute x5 -> x10, waiting for transfers between devices: 34.1 us -> 18.4 us  [the longest x6 10.9 us: shards(): arrivals[c].append(lax.ppermute(carried[c], 'layer', route))]
    pallas_call x5 -> x10, Pallas kernels: 16.2 us -> 8.81 us  [the longest x1 2.57 us: maps(): pl.pallas_call(maps_kernel, in_specs=[in_smem()] + [in_vmem()] * 3, out_s...]
    ppermute x5 -> x10, starting transfers between devices: 3.99 us -> 9.07 us  [the longest x6 5.39 us: shards(): arrivals[c].append(lax.ppermute(carried[c], 'layer', route))]
    unnamed x10 -> x12, local copies, waits for them, and re-layouts: 2.14 us -> 0.03 us
    add x1 -> x0, other arithmetic: 1.71 us -> none  [shards(): arrived = arrived + incoming]
    concatenate x1 -> x0, other arithmetic: 1.05 us -> none  [shards(): jnp.concatenate([jnp.where(first, got, passed), jnp.where(first, passed,...]
  transfers between devices with their start and end apart: 7 -> 12, of which waited for: 4 -> 7; matrix products, arithmetic and copies ran while one was open for 1% -> 0% of each run, Pallas kernels for 17% -> 33%
where the time goes in v2:
time: 68.4 us; the launch traced here: 68.1 us
  waiting for transfers between devices  31.6 us (46%)
  Pallas kernels  24.1 us (35%)
  starting transfers between devices  9.67 us (14%)
  local copies, waits for them, and re-layouts  1.79 us (3%)
  between operations  0.86 us (1%)
    pallas_call x1, Pallas kernels, fine_jump(): pl.pallas_call(fine_kernel, in_specs=[in_smem(), in_smem(), in_vmem(), in...  15.3 us
    ppermute x1, waiting for transfers between devices, shards(): got = lax.ppermute(mine, 'layer', partners)  13.1 us
    ppermute x6, waiting for transfers between devices, shards(): arrivals[c].append(lax.ppermute(carried[c], 'layer', route))  10.9 us
    ppermute x6, starting transfers between devices, shards(): arrivals[c].append(lax.ppermute(carried[c], 'layer', route))  5.39 us
    ppermute x2, waiting for transfers between devices, shards(): pieces += [head, lax.ppermute(out, 'layer', partners), kept[c], sent[c]]  4.83 us
    ppermute x2, waiting for transfers between devices, shards(): received = [lax.ppermute(piece, 'layer', partners) for piece in sent]  2.73 us
    pallas_call x1, Pallas kernels, maps(): pl.pallas_call(maps_kernel, in_specs=[in_smem()] + [in_vmem()] * 3, out_s...  2.57 us
    ppermute x2, starting transfers between devices, shards(): received = [lax.ppermute(piece, 'layer', partners) for piece in sent]  2.09 us
  transfers between devices with their start and end apart: 12, of which 7 were waited for; matrix products, arithmetic and copies ran while one was open for 0% of the time, Pallas kernels for 33%

profile of v2, /device:TPU:26, one launch (start us, length us, event | category | flops | bytes accessed | tf_op | source)
XLA Modules:
  0.0 68.1 jit_solution(14601210570724561733)
XLA Ops:
  0.6 1.1 %dynamic-slice_bitcast_fusion = f32[256,512]{1,0:T(8,128)S(1)} fusion(f32[1,512,512]{2,1,0:T(8,128)} %surrogate.1, s32[]{:T(128)S(6)} %select_n.16), kind=kLoop, calls=%fused_computation | loop fusion | bytes 1048580 | tf_op jit(solution)/shard_map/dynamic_slice | solution.py:307
  2.3 13.1 %collective-permute-done.got = f32[256,512]{1,0:T(8,128)S(1)} collective-permute-done((f32[256,512]{1,0:T(8,128)S(1)}, f32[256,512]{1,0:T(8,128)S(1)}, u32[]{:S(2)}, u32[]{:S(2)}) %collective-permute-start) | collective-permute-done | bytes 524320 | tf_op jit(solution)/shard_map/ppermute | solution.py:308
  15.5 15.3 %shard_map.96 = (f32[64,512]{1,0:T(8,128)}, f32[64,512]{1,0:T(8,128)}, f32[64,512]{1,0:T(8,128)}, f32[64,512]{1,0:T(8,128)}) custom-call(s32[1]{0:T(128)} %bitcast.position, s32[2]{0:T(128)} %lengths.1, f32[1,256,512]{2,1,0:T(8,128)} %start.3, f32[1,512]{1,0:T(1,128)} %gain.1, f32[1,512,512]{2,1,0:T(8,128)} %surrogate.1, bf16[1,512,1536]{2,1,0:T(8,128)(2,1)} %w_qkv.1, ...), custom_call_target="tpu_custom_call" | custom-call | flops 6442450944 | bytes 6291456 | tf_op jit(solution)/shard_map/pallas_call | solution.py:143
  30.8 0.6 collective-permute-start.2
  31.4 1.5 %collective-permute-start.7 = (f32[64,512]{1,0:T(8,128)}, f32[64,512]{1,0:T(8,128)S(1)}, u32[]{:S(2)}, u32[]{:S(2)}) collective-permute-start(f32[64,512]{1,0:T(8,128)} %get-tuple-element.33.rest_7_), channel_id=1, source_target_pairs={{0,4},{4,0},{8,12},{12,8},{16,20},{20,16},{24,28},{28,24},{1,5},{5... | collective-permute-start | bytes 393224 | tf_op jit(solution)/shard_map/ppermute | solution.py:314
  33.0 2.6 %shard_map.95 = (bf16[512,512]{1,0:T(8,128)(2,1)S(1)}, bf16[512,512]{1,0:T(8,128)(2,1)S(1)}, bf16[512,512]{1,0:T(8,128)(2,1)S(1)}, bf16[512,512]{1,0:T(8,128)(2,...) custom-call(s32[2]{0:T(128)S(1)} %pad_add_fusion.parity, ...), custom_call_target="tpu_custom_call" | custom-call | tf_op jit(solution)/shard_map/pallas_call | solution.py:201
  35.5 1.9 %collective-permute-done.2.received = f32[64,512]{1,0:T(8,128)S(1)} collective-permute-done((f32[64,512]{1,0:T(8,128)}, f32[64,512]{1,0:T(8,128)S(1)}, u32[]{:S(2)}, u32[]{:S(2)}) %collective-permute-start.2) | collective-permute-done | bytes 131104 | tf_op jit(solution)/shard_map/ppermute | solution.py:314
  37.4 0.8 %shard_map.97.joined = f32[64,512]{1,0:T(8,128)S(1)} custom-call(s32[2]{0:T(128)S(1)} %pad_add_fusion.parity, f32[64,512]{1,0:T(8,128)S(1)} %copy-done.1, f32[64,512]{1,0:T(8,128)S(1)} %collective-permute-done.2.received, bf16[512,512]{1,0:T(8,128)(2,1)S(1)} %get-tuple-element.26.odd_high, bf16[512,512]{1,0:T(8,128)(2,1)S(1)} %get-tuple-element.27.odd_low), custom_call_target="tpu_custom_call" | custom-call | tf_op jit(solution)/shard_map/pallas_call | solution.py:219
  38.3 0.7 collective-permute-start.3
  39.0 0.8 %collective-permute-done.7.received = f32[64,512]{1,0:T(8,128)S(1)} collective-permute-done((f32[64,512]{1,0:T(8,128)}, f32[64,512]{1,0:T(8,128)S(1)}, u32[]{:S(2)}, u32[]{:S(2)}) %collective-permute-start.7) | collective-permute-done | bytes 131104 | tf_op jit(solution)/shard_map/ppermute | solution.py:314
  39.8 0.8 %shard_map.101.joined = f32[64,512]{1,0:T(8,128)S(1)} custom-call(s32[2]{0:T(128)S(1)} %pad_add_fusion.parity, f32[64,512]{1,0:T(8,128)S(1)} %copy-done.2, f32[64,512]{1,0:T(8,128)S(1)} %collective-permute-done.7.received, bf16[512,512]{1,0:T(8,128)(2,1)S(1)} %get-tuple-element.26.odd_high, bf16[512,512]{1,0:T(8,128)(2,1)S(1)} %get-tuple-element.27.odd_low), custom_call_target="tpu_custom_call" | custom-call | tf_op jit(solution)/shard_map/pallas_call | solution.py:219
  40.7 0.7 collective-permute-start.8
  41.6 0.7 collective-permute-start.4
  42.6 0.7 collective-permute-start.9
  43.6 1.4 %collective-permute-start.5 = (f32[64,512]{1,0:T(8,128)S(1)}, f32[64,512]{1,0:T(8,128)S(1)}, u32[]{:S(2)}, u32[]{:S(2)}) collective-permute-start(f32[64,512]{1,0:T(8,128)S(1)} %shard_map.99), channel_id=1, source_target_pairs={{16,24},{20,28},{17,25},{21,29},{18,26},{22,30},{19,27},{23,31}} | collective-permute-start | bytes 393224 | tf_op jit(solution)/shard_map/ppermute | solution.py:324
  45.4 1.3 %collective-permute-start.10 = (f32[64,512]{1,0:T(8,128)S(1)}, f32[64,512]{1,0:T(8,128)S(1)}, u32[]{:S(2)}, u32[]{:S(2)}) collective-permute-start(f32[64,512]{1,0:T(8,128)S(1)} %shard_map.103), channel_id=1, source_target_pairs={{16,24},{20,28},{17,25},{21,29},{18,26},{22,30},{19,27},{23,31}} | collective-permute-start | bytes 393224 | tf_op jit(solution)/shard_map/ppermute | solution.py:324
  46.7 10.3 %collective-permute-done.5.arrivals_and_outs_2_ = f32[64,512]{1,0:T(8,128)S(1)} collective-permute-done((f32[64,512]{1,0:T(8,128)S(1)}, f32[64,512]{1,0:T(8,128)S(1)}, u32[]{:S(2)}, u32[]{:S(2)}) %collective-permute-start.5) | collective-permute-done | bytes 131104 | tf_op jit(solution)/shard_map/ppermute | solution.py:324
  57.0 0.8 %shard_map.100 = (f32[64,512]{1,0:T(8,128)S(1)}, f32[64,512]{1,0:T(8,128)S(1)}) custom-call(s32[2]{0:T(128)S(1)} %pad_add_fusion.parity, f32[64,512]{1,0:T(8,128)S(1)} %copy-done.1, f32[64,512]{1,0:T(8,128)S(1)} %collective-permute-done.2.received, bf16[512,512]{1,0:T(8,128)(2,1)S(1)} %get-tuple-element.24.even_high, ...), custom_call_target="tpu_custom_call" | custom-call | tf_op jit(solution)/shard_map/pallas_call | solution.py:255
  58.9 0.8 %shard_map.104 = (f32[64,512]{1,0:T(8,128)S(1)}, f32[64,512]{1,0:T(8,128)S(1)}) custom-call(s32[2]{0:T(128)S(1)} %pad_add_fusion.parity, f32[64,512]{1,0:T(8,128)S(1)} %copy-done.2, f32[64,512]{1,0:T(8,128)S(1)} %collective-permute-done.7.received, bf16[512,512]{1,0:T(8,128)(2,1)S(1)} %get-tuple-element.24.even_high, ...), custom_call_target="tpu_custom_call" | custom-call | tf_op jit(solution)/shard_map/pallas_call | solution.py:255
  59.8 1.1 %collective-permute-start.11 = (f32[64,512]{1,0:T(8,128)S(1)}, f32[64,512]{1,0:T(8,128)S(1)}, u32[]{:S(2)}, u32[]{:S(2)}) collective-permute-start(f32[64,512]{1,0:T(8,128)S(1)} %get-tuple-element.35), channel_id=1, source_target_pairs={{0,4},{4,0},{8,12},{12,8},{16,20},{20,16},{24,28},{28,24},{1,5},{5... | collective-permute-start | bytes 393224 | tf_op jit(solution)/shard_map/ppermute | solution.py:330
  60.9 3.2 %collective-permute-done.6.rest_1_ = f32[64,512]{1,0:T(8,128)S(1)} collective-permute-done((f32[64,512]{1,0:T(8,128)S(1)}, f32[64,512]{1,0:T(8,128)S(1)}, u32[]{:S(2)}, u32[]{:S(2)}) %collective-permute-start.6) | collective-permute-done | bytes 131104 | tf_op jit(solution)/shard_map/ppermute | solution.py:330
  64.0 1.7 %collective-permute-done.11.rest_5_ = f32[64,512]{1,0:T(8,128)S(1)} collective-permute-done((f32[64,512]{1,0:T(8,128)S(1)}, f32[64,512]{1,0:T(8,128)S(1)}, u32[]{:S(2)}, u32[]{:S(2)}) %collective-permute-start.11) | collective-permute-done | bytes 131104 | tf_op jit(solution)/shard_map/ppermute | solution.py:330
  65.7 1.7 %shard_map.105 = (f32[1,256,512]{2,1,0:T(8,128)}, f32[256,128]{1,0:T(8,128)S(1)}) custom-call(s32[1]{0:T(128)} %bitcast.position, f32[1,256,512]{2,1,0:T(8,128)S(1)} %copy-done.3, bf16[512,512]{1,0:T(8,128)(2,1)S(1)} %get-tuple-element.20.own_high, bf16[512,512]{1,0:T(8,128)(2,1)S(1)} %get-tuple-element.21.own_low, f32[64,512]{1,0:T(8,128)S(1)} %get-tuple-element.30.rest_0_, ...), custom_call_target="tpu_custom_call" | custom-call | tf_op jit(solution)/shard_map/pallas_call | solution.py:284
  67.4 0.7 slice_reduce_fusion
  (26 shorter events, 3.0 us)
Async XLA Ops:
  1.7 13.7 %collective-permute-start = (f32[256,512]{1,0:T(8,128)S(1)}, f32[256,512]{1,0:T(8,128)S(1)}, u32[]{:S(2)}, u32[]{:S(2)}) collective-permute-start(f32[256,512]{1,0:T(8,128)S(1)} %dynamic-slice_bitcast_fusion), channel_id=1, source_target_pairs={{0,4},{4,0},{8,12},{12,8},{16,20},{20,16},{24,28},{28,24},{1,5},{5... | collective-permute-start | bytes 1572872 | tf_op jit(solution)/shard_map/ppermute | solution.py:308
  15.5 17.5 %collective-permute-start.1 = (f32[256,512]{1,0:T(8,128)S(1)}, f32[256,512]{1,0:T(8,128)}, u32[]{:S(2)}, u32[]{:S(2)}) collective-permute-start(f32[256,512]{1,0:T(8,128)S(1)} %collective-permute-done.got), channel_id=1, source_target_pairs={{0,1},{1,0},{2,3},{3,2},{4,5},{5,4},{6,7},{7,6},{8,9},{9,8},{10,11... | collective-permute-start | bytes 1572872 | tf_op jit(solution)/shard_map/ppermute | solution.py:312
  15.5 17.5 %copy-start = (f32[1,512,512]{2,1,0:T(8,128)S(1)}, f32[1,512,512]{2,1,0:T(8,128)}, u32[]{:S(2)}) copy-start(f32[1,512,512]{2,1,0:T(8,128)} %surrogate.1) | copy-start | bytes 3145732
  30.8 6.7 %copy-start.1 = (f32[64,512]{1,0:T(8,128)S(1)}, f32[64,512]{1,0:T(8,128)}, u32[]{:S(2)}) copy-start(f32[64,512]{1,0:T(8,128)} %get-tuple-element.22.kept.rest_2_) | copy-start | bytes 393220
  30.8 9.0 %copy-start.2 = (f32[64,512]{1,0:T(8,128)S(1)}, f32[64,512]{1,0:T(8,128)}, u32[]{:S(2)}) copy-start(f32[64,512]{1,0:T(8,128)} %get-tuple-element.32.kept.rest_6_) | copy-start | bytes 393220
  30.8 6.6 %collective-permute-start.2 = (f32[64,512]{1,0:T(8,128)}, f32[64,512]{1,0:T(8,128)S(1)}, u32[]{:S(2)}, u32[]{:S(2)}) collective-permute-start(f32[64,512]{1,0:T(8,128)} %get-tuple-element.23.rest_3_), channel_id=1, source_target_pairs={{0,4},{4,0},{8,12},{12,8},{16,20},{20,16},{24,28},{28,24},{1,5},{5... | collective-permute-start | bytes 393224 | tf_op jit(solution)/shard_map/ppermute | solution.py:314
  31.4 8.4 %collective-permute-start.7 = (f32[64,512]{1,0:T(8,128)}, f32[64,512]{1,0:T(8,128)S(1)}, u32[]{:S(2)}, u32[]{:S(2)}) collective-permute-start(f32[64,512]{1,0:T(8,128)} %get-tuple-element.33.rest_7_), channel_id=1, source_target_pairs={{0,4},{4,0},{8,12},{12,8},{16,20},{20,16},{24,28},{28,24},{1,5},{5... | collective-permute-start | bytes 393224 | tf_op jit(solution)/shard_map/ppermute | solution.py:314
  38.3 3.0 %collective-permute-start.3 = (f32[64,512]{1,0:T(8,128)S(1)}, f32[64,512]{1,0:T(8,128)S(1)}, u32[]{:S(2)}, u32[]{:S(2)}) collective-permute-start(f32[64,512]{1,0:T(8,128)S(1)} %shard_map.97.joined), channel_id=1, source_target_pairs={{0,8},{4,12},{1,9},{5,13},{2,10},{6,14},{3,11},{7,15}} | collective-permute-start | bytes 393224 | tf_op jit(solution)/shard_map/ppermute | solution.py:324
  40.7 1.7 %collective-permute-start.8 = (f32[64,512]{1,0:T(8,128)S(1)}, f32[64,512]{1,0:T(8,128)S(1)}, u32[]{:S(2)}, u32[]{:S(2)}) collective-permute-start(f32[64,512]{1,0:T(8,128)S(1)} %shard_map.101.joined), channel_id=1, source_target_pairs={{0,8},{4,12},{1,9},{5,13},{2,10},{6,14},{3,11},{7,15}} | collective-permute-start | bytes 393224 | tf_op jit(solution)/shard_map/ppermute | solution.py:324
  41.6 1.7 %collective-permute-start.4 = (f32[64,512]{1,0:T(8,128)S(1)}, f32[64,512]{1,0:T(8,128)S(1)}, u32[]{:S(2)}, u32[]{:S(2)}) collective-permute-start(f32[64,512]{1,0:T(8,128)S(1)} %shard_map.98), channel_id=1, source_target_pairs={{8,16},{12,20},{9,17},{13,21},{10,18},{14,22},{11,19},{15,23}} | collective-permute-start | bytes 393224 | tf_op jit(solution)/shard_map/ppermute | solution.py:324
  42.6 2.5 %collective-permute-start.9 = (f32[64,512]{1,0:T(8,128)S(1)}, f32[64,512]{1,0:T(8,128)S(1)}, u32[]{:S(2)}, u32[]{:S(2)}) collective-permute-start(f32[64,512]{1,0:T(8,128)S(1)} %shard_map.102), channel_id=1, source_target_pairs={{8,16},{12,20},{9,17},{13,21},{10,18},{14,22},{11,19},{15,23}} | collective-permute-start | bytes 393224 | tf_op jit(solution)/shard_map/ppermute | solution.py:324
  43.6 22.1 %copy-start.3 = (f32[1,256,512]{2,1,0:T(8,128)S(1)}, f32[1,256,512]{2,1,0:T(8,128)}, u32[]{:S(2)}) copy-start(f32[1,256,512]{2,1,0:T(8,128)} %start.3) | copy-start | bytes 1572868
  43.6 22.1 %copy-start.4 = (f32[64,512]{1,0:T(8,128)S(1)}, f32[64,512]{1,0:T(8,128)}, u32[]{:S(2)}) copy-start(f32[64,512]{1,0:T(8,128)} %get-tuple-element.23.rest_3_) | copy-start | bytes 393220
  43.6 22.1 %copy-start.5 = (f32[64,512]{1,0:T(8,128)S(1)}, f32[64,512]{1,0:T(8,128)}, u32[]{:S(2)}) copy-start(f32[64,512]{1,0:T(8,128)} %get-tuple-element.33.rest_7_) | copy-start | bytes 393220
  43.6 13.3 %collective-permute-start.5 = (f32[64,512]{1,0:T(8,128)S(1)}, f32[64,512]{1,0:T(8,128)S(1)}, u32[]{:S(2)}, u32[]{:S(2)}) collective-permute-start(f32[64,512]{1,0:T(8,128)S(1)} %shard_map.99), channel_id=1, source_target_pairs={{16,24},{20,28},{17,25},{21,29},{18,26},{22,30},{19,27},{23,31}} | collective-permute-start | bytes 393224 | tf_op jit(solution)/shard_map/ppermute | solution.py:324
  45.4 13.6 %collective-permute-start.10 = (f32[64,512]{1,0:T(8,128)S(1)}, f32[64,512]{1,0:T(8,128)S(1)}, u32[]{:S(2)}, u32[]{:S(2)}) collective-permute-start(f32[64,512]{1,0:T(8,128)S(1)} %shard_map.103), channel_id=1, source_target_pairs={{16,24},{20,28},{17,25},{21,29},{18,26},{22,30},{19,27},{23,31}} | collective-permute-start | bytes 393224 | tf_op jit(solution)/shard_map/ppermute | solution.py:324
  57.8 6.2 %collective-permute-start.6 = (f32[64,512]{1,0:T(8,128)S(1)}, f32[64,512]{1,0:T(8,128)S(1)}, u32[]{:S(2)}, u32[]{:S(2)}) collective-permute-start(f32[64,512]{1,0:T(8,128)S(1)} %get-tuple-element.31), channel_id=1, source_target_pairs={{0,4},{4,0},{8,12},{12,8},{16,20},{20,16},{24,28},{28,24},{1,5},{5... | collective-permute-start | bytes 393224 | tf_op jit(solution)/shard_map/ppermute | solution.py:330
  59.8 5.9 %collective-permute-start.11 = (f32[64,512]{1,0:T(8,128)S(1)}, f32[64,512]{1,0:T(8,128)S(1)}, u32[]{:S(2)}, u32[]{:S(2)}) collective-permute-start(f32[64,512]{1,0:T(8,128)S(1)} %get-tuple-element.35), channel_id=1, source_target_pairs={{0,4},{4,0},{8,12},{12,8},{16,20},{20,16},{24,28},{28,24},{1,5},{5... | collective-permute-start | bytes 393224 | tf_op jit(solution)/shard_map/ppermute | solution.py:330

commit v3 on v2

v3 whole, which is shorter than its diff:
```python
import functools
import math

import jax
import jax.numpy as jnp
from jax import lax
from jax.experimental import pallas as pl
from jax.experimental.pallas import tpu as pltpu
from jax.sharding import PartitionSpec as P


HEAD_DIM = 64
SEQ = 128
FINE = 4
QUERY_SCALE = math.log2(math.e) / math.sqrt(HEAD_DIM)
CHUNKS = 2
PAIR = 2 * HEAD_DIM
F32 = jnp.float32
BF16 = jnp.bfloat16


def halves_of(a):
    high = a.astype(BF16)
    return high, (a - high.astype(F32)).astype(BF16)


def dot_split(a, b_high, b_low):
    a_high, a_low = halves_of(a)
    rows = a.shape[0]
    both = jnp.dot(jnp.concatenate([a_high, a_low], 0), b_high, preferred_element_type=F32)
    return both[:rows] + (both[rows:] + jnp.dot(a_high, b_low, preferred_element_type=F32))


def params(megabytes):
    return pltpu.CompilerParams(vmem_limit_bytes=megabytes << 20)


def in_vmem():
    return pl.BlockSpec(memory_space=pltpu.VMEM)


def in_place():
    return pl.BlockSpec(memory_space=pltpu.HBM)


def place():
    return lax.axis_index("layer"), lax.axis_index("dp") % 2


def is_even():
    return lax.axis_index("layer") % 2 == 0


def fine_kernel(
    lengths, start, gain, surrogate, w_qkv, w_out, w_up, w_down, *outs_and_scratch
):
    *pieces, begun, scale, limits, w_in, w_back, varying, state, act, qkv, bias, sems = outs_and_scratch
    tokens, width = state.shape
    hidden = w_back.shape[0] - width
    moves = (
        (start.at[0], begun),
        (gain, scale),
        (w_qkv.at[0], w_in.at[:, pl.ds(0, 3 * width)]),
        (lengths, limits),
        (w_up.at[0], w_in.at[:, pl.ds(3 * width, hidden)]),
        (w_out.at[0], w_back.at[pl.ds(0, width), :]),
        (w_down.at[0], w_back.at[pl.ds(width, hidden), :]),
        (surrogate.at[0], varying),
    )
    copies = [
        pltpu.make_async_copy(source, target, sems.at[at])
        for at, (source, target) in enumerate(moves)
    ]
    for copy in copies:
        copy.start()
    query = lax.broadcasted_iota(jnp.int32, (SEQ, SEQ), 0)
    key = lax.broadcasted_iota(jnp.int32, (SEQ, SEQ), 1)
    sequences = tokens // SEQ
    low = lax.broadcasted_iota(jnp.int32, (SEQ, PAIR), 1) < HEAD_DIM
    zeros = jnp.zeros((SEQ, PAIR), BF16)
    ones = jnp.ones((SEQ, PAIR), BF16)

    def by_head(block):
        return jnp.concatenate([jnp.where(low, block, zeros), jnp.where(low, zeros, block)], 0)

    counts = by_head(0.5 * ones)
    chunk = width
    curve = math.sqrt(2 / math.pi)
    copies[0].wait()
    copies[1].wait()
    state[...] = begun[...]

    def substep(first):
        x = state[...]
        mean_square = jnp.mean(x * x, axis=1, keepdims=True)
        normed = (x * lax.rsqrt(mean_square + 1e-06) * scale[...]).astype(BF16)

        if first:
            copies[2].wait()

        for n in range(0, 3 * width, chunk):
            packed = jnp.dot(normed, w_in[:, n : n + chunk], preferred_element_type=F32)
            if n < width:
                packed = packed * QUERY_SCALE
            qkv[:, n : n + chunk] = packed.astype(BF16)

        if first:
            copies[3].wait()
            for s in range(sequences):
                allowed = (key <= query) & (key < limits[s])
                bias[pl.ds(s * SEQ, SEQ), :] = jnp.where(allowed, 0.0, -1e30).astype(F32)

        for s in range(sequences):
            rows = pl.ds(s * SEQ, SEQ)
            mask = bias[rows, :]
            masks = jnp.concatenate([mask, mask], 0)
            for at in range(0, width, PAIR):
                queries = qkv[rows, at : at + PAIR]
                keys = qkv[rows, width + at : width + at + PAIR]
                values = qkv[rows, 2 * width + at : 2 * width + at + PAIR]
                scores = lax.dot_general(
                    by_head(queries), keys, (((1,), (1,)), ((), ())), preferred_element_type=F32
                ) + masks
                top = jnp.max(scores, axis=-1, keepdims=True)
                weights = jnp.exp2(scores - top).astype(BF16)
                pair = jnp.concatenate([weights[:SEQ], weights[SEQ:]], 1)
                both = jnp.dot(
                    pair, jnp.concatenate([by_head(values), counts], 1), preferred_element_type=F32
                )
                act[rows, at : at + PAIR] = (both[:, :PAIR] / both[:, PAIR:]).astype(BF16)

        if first:
            copies[4].wait()

        for n in range(0, hidden, chunk):
            u = jnp.dot(
                normed, w_in[:, 3 * width + n : 3 * width + n + chunk], preferred_element_type=F32
            )
            gelu = u + u * jnp.tanh(u * (curve + (curve * 0.044715) * (u * u)))
            act[:, width + n : width + n + chunk] = gelu.astype(BF16)

        if first:
            copies[5].wait()
            copies[6].wait()

        state[...] = x + jnp.dot(act[...], w_back[...], preferred_element_type=F32) * (0.5 / FINE)

    substep(True)

    @pl.loop(1, FINE)
    def _(_):
        substep(False)

    copies[7].wait()
    layer, _ = place()
    share = jnp.where(layer == 0, 0.0, 1.0).astype(F32)
    high, low_part = halves_of(0.3 * varying[...])
    through = 0.9 * begun[...] + dot_split(begun[...], high, low_part)
    state[...] = state[...] - share * through
    mine = layer % 2
    half = pieces[0].shape[0]
    for at in range(len(pieces) // 2):
        for piece, part in ((pieces[2 * at], mine), (pieces[2 * at + 1], 1 - mine)):
            piece[...] = state[pl.ds(pl.multiple_of((2 * at + part) * half, half), half), :]


def fine_jump(chunks, lengths, start, gain, surrogate, w_qkv, w_out, w_up, w_down):
    tokens, width = start.shape[1:]
    hidden = w_up.shape[2]
    half = jax.ShapeDtypeStruct((tokens // (2 * chunks), width), F32)
    return pl.pallas_call(
        fine_kernel,
        in_specs=[in_place()] * 8,
        out_specs=[in_vmem()] * (2 * chunks),
        out_shape=[half] * (2 * chunks),
        scratch_shapes=[
            pltpu.VMEM((tokens, width), F32),
            pltpu.VMEM(gain.shape, F32),
            pltpu.SMEM(lengths.shape, jnp.int32),
            pltpu.VMEM((width, 3 * width + hidden), BF16),
            pltpu.VMEM((width + hidden, width), BF16),
            pltpu.VMEM((width, width), F32),
            pltpu.VMEM((tokens, width), F32),
            pltpu.VMEM((tokens, width + hidden), BF16),
            pltpu.VMEM((tokens, 3 * width), BF16),
            pltpu.VMEM((tokens, SEQ), F32),
            pltpu.SemaphoreType.DMA((8,)),
        ],
        cost_estimate=pl.CostEstimate(
            flops=2 * FINE * tokens * width * (4 * width + 2 * hidden),
            transcendentals=FINE * tokens * hidden,
            bytes_accessed=2 * width * (4 * width + 2 * hidden),
        ),
        compiler_params=params(62),
    )(lengths, start, gain, surrogate, w_qkv, w_out, w_up, w_down)


def partner_map(got, passed, other):
    core = lax.axis_index("dp") % 2

    @pl.when(core == 0)
    def _():
        other[...] = 0.3 * got[0]

    @pl.when(core != 0)
    def _():
        other[...] = 0.3 * passed[0]


def odd_kernel(own, got, passed, odd_high, odd_low, other):
    even = is_even()

    @pl.when(even)
    def _():
        partner_map(got, passed, other)

    @pl.when(jnp.logical_not(even))
    def _():
        other[...] = 0.3 * own[0]

    odd_high[...], odd_low[...] = halves_of(other[...])


def odd_map(own, got, passed):
    width = own.shape[1]
    square = jax.ShapeDtypeStruct((width, width), BF16)
    return pl.pallas_call(
        odd_kernel,
        in_specs=[in_vmem()] * 3,
        out_specs=[in_vmem()] * 2,
        out_shape=[square] * 2,
        scratch_shapes=[pltpu.VMEM((width, width), F32)],
        compiler_params=params(8),
    )(own, got, passed)


def maps_kernel(
    own, got, passed, odd_high, odd_low, own_high, own_low, even_high, even_low, both_high, both_low, other
):
    even = is_even()

    @pl.when(even)
    def _():
        other[...] = 0.3 * own[0]

    @pl.when(jnp.logical_not(even))
    def _():
        partner_map(got, passed, other)

    own_high[...], own_low[...] = halves_of(0.3 * own[0])
    first = other[...]
    even_high[...], even_low[...] = halves_of(first)
    second = odd_high[...].astype(F32) + odd_low[...].astype(F32)
    product = 0.9 * (first + second) + dot_split(first, odd_high[...], odd_low[...])
    both_high[...], both_low[...] = halves_of(product)


def maps(own, got, passed, odd):
    width = own.shape[1]
    square = jax.ShapeDtypeStruct((width, width), BF16)
    return pl.pallas_call(
        maps_kernel,
        in_specs=[in_vmem()] * 5,
        out_specs=[in_vmem()] * 6,
        out_shape=[square] * 6,
        scratch_shapes=[pltpu.VMEM((width, width), F32)],
        compiler_params=params(14),
    )(own, got, passed, *odd)


def join_kernel(kept, received, odd_high, odd_low, out):
    even = is_even()
    first = jnp.where(even, kept[...], received[...])
    second = jnp.where(even, received[...], kept[...])
    out[...] = second + (0.9 * first + dot_split(first, odd_high[...], odd_low[...]))


def join(kept, received, odd):
    return pl.pallas_call(
        join_kernel,
        in_specs=[in_vmem()] * 4,
        out_specs=in_vmem(),
        out_shape=jax.ShapeDtypeStruct(kept.shape, F32),
        compiler_params=params(8),
    )(kept, received, *odd)


def hop_kernel(incoming, joined, both_high, both_low, out):
    state = incoming[...]
    out[...] = joined[...] + (0.81 * state + dot_split(state, both_high[...], both_low[...]))


def hop(incoming, joined, both):
    return pl.pallas_call(
        hop_kernel,
        in_specs=[in_vmem()] * 4,
        out_specs=in_vmem(),
        out_shape=jax.ShapeDtypeStruct(incoming.shape, F32),
        compiler_params=params(8),
    )(incoming, joined, *both)


def turn_kernel(kept, received, even_high, even_low, *arrivals_and_outs):
    *arrivals, head, out = arrivals_and_outs
    state = functools.reduce(jnp.add, [arrival[...] for arrival in arrivals])
    even = is_even()
    first = jnp.where(even, kept[...], received[...])
    after = first + (0.9 * state + dot_split(state, even_high[...], even_low[...]))
    head[...] = jnp.where(even, state, after)
    out[...] = jnp.where(even, after, state)


def turn(kept, received, even, arrivals):
    shape = jax.ShapeDtypeStruct(kept.shape, F32)
    return pl.pallas_call(
        turn_kernel,
        in_specs=[in_vmem()] * (4 + len(arrivals)),
        out_specs=[in_vmem()] * 2,
        out_shape=[shape, shape],
        compiler_params=params(8),
    )(kept, received, *even, *arrivals)


def part_of(row, ahead, jump, start, own_high, own_low):
    half, width = ahead.shape
    state = ahead[...]
    new = jump[...] + (0.9 * state + dot_split(state, own_high[...], own_low[...]))
    difference = state - start[0, pl.ds(pl.multiple_of(row * half, half), half), :]
    total = lax.dot_general(
        jnp.ones((8, width), F32), difference * difference, (((1,), (1,)), ((), ())),
        precision=lax.Precision.HIGHEST, preferred_element_type=F32,
    )
    return new, jnp.sqrt(total * (1.0 / width))


def part_kernel(at, other, ahead, jump, start, own_high, own_low, new, change):
    row = 2 * at + (lax.axis_index("layer") + other) % 2
    new[...], change[...] = part_of(row, ahead, jump, start, own_high, own_low)


def part(at, other, ahead, jump, start, own):
    half, width = ahead.shape
    return pl.pallas_call(
        functools.partial(part_kernel, at, other),
        in_specs=[in_vmem()] * 5,
        out_specs=[in_vmem()] * 2,
        out_shape=[
            jax.ShapeDtypeStruct((half, width), F32), jax.ShapeDtypeStruct((8, half), F32)
        ],
        compiler_params=params(8),
    )(ahead, jump, start, *own)


def close_kernel(count, ahead, jump, start, own_high, own_low, *rest):
    *done, out, change = rest
    half = ahead.shape[0]
    layer = lax.axis_index("layer")
    even = layer % 2 == 0
    share = jnp.where(layer == 0, 0.0, 1.0).astype(F32)
    last = part_of(2 * count - 1 - layer % 2, ahead, jump, start, own_high, own_low)
    done = [(done[at][...], done[at + 1][...]) for at in range(0, len(done), 2)] + [last]
    for at in range(count):
        (mine, mine_change), (other, other_change) = done[2 * at], done[2 * at + 1]
        out[0, pl.ds(2 * at * half, half), :] = jnp.where(even, mine, other)
        out[0, pl.ds((2 * at + 1) * half, half), :] = jnp.where(even, other, mine)
        row = jnp.where(
            even,
            jnp.concatenate([mine_change, other_change], 1),
            jnp.concatenate([other_change, mine_change], 1),
        )
        change[:, pl.ds(2 * at * half, 2 * half)] = share * row[:1]


def close(count, ahead, jump, start, own, done):
    tokens, width = start.shape[1:]
    return pl.pallas_call(
        functools.partial(close_kernel, count),
        in_specs=[in_vmem()] * (5 + len(done)),
        out_specs=[in_vmem()] * 2,
        out_shape=[
            jax.ShapeDtypeStruct((1, tokens, width), F32),
            jax.ShapeDtypeStruct((1, tokens), F32),
        ],
        compiler_params=params(12),
    )(ahead, jump, start, *own, *done)


def shards(old_heads, surrogate, norm_gain, w_qkv, w_out, w_up, w_down, lengths):
    layers = lax.axis_size("layer")
    batches = lax.axis_size("dp")
    partners = [(i, i ^ 1) for i in range(layers)]
    ports = [
        (i * batches + j, (i ^ 1) * batches + j) for i in range(layers) for j in range(0, batches, 2)
    ]
    got = lax.ppermute(surrogate, ("layer", "dp"), ports)
    pieces = fine_jump(CHUNKS, lengths, old_heads, norm_gain, surrogate, w_qkv, w_out, w_up, w_down)
    kept, sent = pieces[::2], pieces[1::2]
    spans = range(CHUNKS)
    received = []
    for c in spans:
        received.append(lax.ppermute(sent[c], "layer", partners))
    passed = lax.ppermute(got, "dp", [(i, i + 1) for i in range(0, batches - 1, 2)])
    odd = odd_map(surrogate, got, passed)
    split = maps(surrogate, got, passed, odd)
    own, even, both = split[0:2], split[2:4], split[4:6]
    joined = [join(kept[c], received[c], odd) for c in spans]
    carried = joined
    arrivals = [[] for c in spans]
    for at in range(0, layers - 2, 2):
        route = [(at, at + 2), (at + 1, at + 3)]
        for c in spans:
            arrivals[c].append(lax.ppermute(carried[c], "layer", route))
        if at < layers - 4:
            carried = [hop(arrivals[c][-1], joined[c], both) for c in spans]
    heads, returned = [], []
    for c in spans:
        head, out = turn(kept[c], received[c], even, arrivals[c])
        heads.append(head)
        returned.append(lax.ppermute(out, "layer", partners))
    done = []
    for c in spans:
        done += part(c, 0, heads[c], kept[c], old_heads, own)
        if c + 1 < CHUNKS:
            done += part(c, 1, returned[c], sent[c], old_heads, own)
    return close(CHUNKS, returned[-1], sent[-1], old_heads, own, done)


def solution(mesh):
    in_specs = (
        P("layer", "dp", None),
        P("layer", None, None),
        P("layer", None),
        P("layer", None, None),
        P("layer", None, None),
        P("layer", None, None),
        P("layer", None, None),
        P("dp"),
    )
    out_specs = (P("layer", "dp", None), P("layer", "dp"))
    return jax.shard_map(shards, mesh=mesh, in_specs=in_specs, out_specs=out_specs, check_vma=False)
```

time: 68.4 us -> 65 us (0.950)
  waiting for transfers between devices: 31.6 us -> 26.9 us
  starting transfers between devices: 9.67 us -> 13.9 us
  local copies, waits for them, and re-layouts: 1.79 us -> 0.03 us
  Pallas kernels: 24.1 us -> 22.7 us
    ppermute x6, starting transfers between devices: 4.28 us -> 8.48 us  [the longest x1 2.58 us: shards(): got = lax.ppermute(surrogate, ('layer', 'dp'), ports)]
    ppermute x6, waiting for transfers between devices: 10.9 us -> 7.56 us  [shards(): arrivals[c].append(lax.ppermute(carried[c], 'layer', route))]
    ppermute x6, waiting for transfers between devices: 20.7 us -> 19.3 us  [the longest x1 14.6 us: shards(): got = lax.ppermute(surrogate, ('layer', 'dp'), ports)]
    pallas_call x7 -> x11, Pallas kernels: 22.9 us -> 21.6 us  [the longest x1 13.1 us: fine_jump(): pl.pallas_call(fine_kernel, in_specs=[in_place()] * 8, out_specs=[in_vmem...]
    dynamic_slice x1 -> x0, local copies, waits for them, and re-layouts: 1.08 us -> none  [shards(): mine = lax.dynamic_slice_in_dim(surrogate[0], core * part, part, 0)]
where the time goes in v3:
time: 65 us; the launch traced here: 64.4 us
  waiting for transfers between devices  26.9 us (41%)
  Pallas kernels  22.7 us (35%)
  starting transfers between devices  13.9 us (21%)
  between operations  0.87 us (1%)
    ppermute x1, waiting for transfers between devices, shards(): got = lax.ppermute(surrogate, ('layer', 'dp'), ports)  14.6 us
    pallas_call x1, Pallas kernels, fine_jump(): pl.pallas_call(fine_kernel, in_specs=[in_place()] * 8, out_specs=[in_vmem...  13.1 us
    ppermute x6, waiting for transfers between devices, shards(): arrivals[c].append(lax.ppermute(carried[c], 'layer', route))  7.56 us
    ppermute x6, starting transfers between devices, shards(): arrivals[c].append(lax.ppermute(carried[c], 'layer', route))  5.39 us
    pallas_call x1, Pallas kernels, maps(): pl.pallas_call(maps_kernel, in_specs=[in_vmem()] * 5, out_specs=[in_vmem(...  3.12 us
    ppermute x2, waiting for transfers between devices, shards(): returned.append(lax.ppermute(out, 'layer', partners))  2.98 us
    ppermute x1, starting transfers between devices, shards(): got = lax.ppermute(surrogate, ('layer', 'dp'), ports)  2.58 us
    ppermute x1, starting transfers between devices, shards(): lax.ppermute(got, 'dp', [(i, i + 1) for i in range(0, batches - 1, 2)])  2.25 us
  transfers between devices with their start and end apart: 12, of which 7 were waited for; matrix products, arithmetic and copies ran while one was open for 0% of the time, Pallas kernels for 33%

profile of v3, /device:TPU:26, one launch (start us, length us, event | category | flops | bytes accessed | tf_op | source)
XLA Modules:
  0.0 64.4 jit_solution(3532100304491866655)
XLA Ops:
  0.6 2.6 %collective-permute-start.1 = (f32[1,512,512]{2,1,0:T(8,128)}, f32[1,512,512]{2,1,0:T(8,128)}, u32[]{:S(2)}, u32[]{:S(2)}) collective-permute-start(f32[1,512,512]{2,1,0:T(8,128)} %own.3), channel_id=1, source_target_pairs={{0,4},{2,6},{4,0},{6,2},{8,12},{10,14},{12,8},{14,10},{16,20},{18,... | collective-permute-start | bytes 3145736 | tf_op jit(solution)/shard_map/ppermute | solution.py:395
  3.2 14.6 %collective-permute-done.1.got = f32[1,512,512]{2,1,0:T(8,128)} collective-permute-done((f32[1,512,512]{2,1,0:T(8,128)}, f32[1,512,512]{2,1,0:T(8,128)}, u32[]{:S(2)}, u32[]{:S(2)}) %collective-permute-start.1) | collective-permute-done | bytes 1048608 | tf_op jit(solution)/shard_map/ppermute | solution.py:395
  17.8 2.3 %collective-permute-start.2 = (f32[1,512,512]{2,1,0:T(8,128)}, f32[1,512,512]{2,1,0:T(8,128)}, u32[]{:S(2)}, u32[]{:S(2)}) collective-permute-start(f32[1,512,512]{2,1,0:T(8,128)} %collective-permute-done.1.got), channel_id=1, source_target_pairs={{0,1},{2,3},{4,5},{6,7},{8,9},{10,11},{12,13},{14,15},{16,17},{18,... | collective-permute-start | bytes 3145736 | tf_op jit(solution)/shard_map/ppermute | solution.py:402
  20.0 13.1 %shard_map.95 = (f32[64,512]{1,0:T(8,128)}, f32[64,512]{1,0:T(8,128)}, f32[64,512]{1,0:T(8,128)}, f32[64,512]{1,0:T(8,128)}) custom-call(s32[2]{0:T(128)} %lengths.1, f32[1,256,512]{2,1,0:T(8,128)} %start.9, f32[1,512]{1,0:T(1,128)} %gain.1, f32[1,512,512]{2,1,0:T(8,128)} %own.3, bf16[1,512,1536]{2,1,0:T(8,128)(2,1)} %w_qkv.1, bf16[1,512,512]{2,1,0:T(8,128)(2,1)} %w_out.1, ...), custom_call_target="tpu_custom_call" | custom-call | flops 6442450944 | bytes 6291456 | tf_op jit(solution)/shard_map/pallas_call | solution.py:171
  33.2 0.6 collective-permute-start.7
  33.8 1.5 %collective-permute-start = (f32[64,512]{1,0:T(8,128)}, f32[64,512]{1,0:T(8,128)S(1)}, u32[]{:S(2)}, u32[]{:S(2)}) collective-permute-start(f32[64,512]{1,0:T(8,128)} %get-tuple-element.25.jump), channel_id=1, source_target_pairs={{0,4},{4,0},{8,12},{12,8},{16,20},{20,16},{24,28},{28,24},{1,5},{5... | collective-permute-start | bytes 393224 | tf_op jit(solution)/shard_map/ppermute | solution.py:401
  35.3 1.8 %shard_map.96 = (bf16[512,512]{1,0:T(8,128)(2,1)S(1)}, bf16[512,512]{1,0:T(8,128)(2,1)S(1)}) custom-call(f32[1,512,512]{2,1,0:T(8,128)S(1)} %copy-done.1, f32[1,512,512]{2,1,0:T(8,128)} %collective-permute-done.1.got, f32[1,512,512]{2,1,0:T(8,128)} %collective-permute-done.2.passed), custom_call_target="tpu_custom_call" | custom-call | tf_op jit(solution)/shard_map/pallas_call | solution.py:227
  37.0 1.4 %collective-permute-done.7.received = f32[64,512]{1,0:T(8,128)S(1)} collective-permute-done((f32[64,512]{1,0:T(8,128)}, f32[64,512]{1,0:T(8,128)S(1)}, u32[]{:S(2)}, u32[]{:S(2)}) %collective-permute-start.7) | collective-permute-done | bytes 131104 | tf_op jit(solution)/shard_map/ppermute | solution.py:401
  38.7 0.7 %collective-permute-start.8 = (f32[64,512]{1,0:T(8,128)S(1)}, f32[64,512]{1,0:T(8,128)S(1)}, u32[]{:S(2)}, u32[]{:S(2)}) collective-permute-start(f32[64,512]{1,0:T(8,128)S(1)} %shard_map.102.joined), channel_id=1, source_target_pairs={{0,8},{4,12},{1,9},{5,13},{2,10},{6,14},{3,11},{7,15}} | collective-permute-start | bytes 393224 | tf_op jit(solution)/shard_map/ppermute | solution.py:412
  39.4 0.4 collective-permute-done.received
  40.1 0.7 %collective-permute-start.3 = (f32[64,512]{1,0:T(8,128)S(1)}, f32[64,512]{1,0:T(8,128)S(1)}, u32[]{:S(2)}, u32[]{:S(2)}) collective-permute-start(f32[64,512]{1,0:T(8,128)S(1)} %shard_map.98.joined), channel_id=1, source_target_pairs={{0,8},{4,12},{1,9},{5,13},{2,10},{6,14},{3,11},{7,15}} | collective-permute-start | bytes 393224 | tf_op jit(solution)/shard_map/ppermute | solution.py:412
  40.8 3.1 %shard_map.97 = (bf16[512,512]{1,0:T(8,128)(2,1)S(1)}, bf16[512,512]{1,0:T(8,128)(2,1)S(1)}, bf16[512,512]{1,0:T(8,128)(2,1)S(1)}, bf16[512,512]{1,0:T(8,128)(2,...) custom-call(f32[1,512,512]{2,1,0:T(8,128)S(1)} %copy-done.1, ...), custom_call_target="tpu_custom_call" | custom-call | tf_op jit(solution)/shard_map/pallas_call | solution.py:261
  44.2 0.7 %collective-permute-start.9 = (f32[64,512]{1,0:T(8,128)S(1)}, f32[64,512]{1,0:T(8,128)S(1)}, u32[]{:S(2)}, u32[]{:S(2)}) collective-permute-start(f32[64,512]{1,0:T(8,128)S(1)} %shard_map.103), channel_id=1, source_target_pairs={{8,16},{12,20},{9,17},{13,21},{10,18},{14,22},{11,19},{15,23}} | collective-permute-start | bytes 393224 | tf_op jit(solution)/shard_map/ppermute | solution.py:412
  45.2 0.7 %collective-permute-start.4 = (f32[64,512]{1,0:T(8,128)S(1)}, f32[64,512]{1,0:T(8,128)S(1)}, u32[]{:S(2)}, u32[]{:S(2)}) collective-permute-start(f32[64,512]{1,0:T(8,128)S(1)} %shard_map.99), channel_id=1, source_target_pairs={{8,16},{12,20},{9,17},{13,21},{10,18},{14,22},{11,19},{15,23}} | collective-permute-start | bytes 393224 | tf_op jit(solution)/shard_map/ppermute | solution.py:412
  46.2 1.4 %collective-permute-start.10 = (f32[64,512]{1,0:T(8,128)S(1)}, f32[64,512]{1,0:T(8,128)S(1)}, u32[]{:S(2)}, u32[]{:S(2)}) collective-permute-start(f32[64,512]{1,0:T(8,128)S(1)} %shard_map.104), channel_id=1, source_target_pairs={{16,24},{20,28},{17,25},{21,29},{18,26},{22,30},{19,27},{23,31}} | collective-permute-start | bytes 393224 | tf_op jit(solution)/shard_map/ppermute | solution.py:412
  48.0 1.3 %collective-permute-start.5 = (f32[64,512]{1,0:T(8,128)S(1)}, f32[64,512]{1,0:T(8,128)S(1)}, u32[]{:S(2)}, u32[]{:S(2)}) collective-permute-start(f32[64,512]{1,0:T(8,128)S(1)} %shard_map.100), channel_id=1, source_target_pairs={{16,24},{20,28},{17,25},{21,29},{18,26},{22,30},{19,27},{23,31}} | collective-permute-start | bytes 393224 | tf_op jit(solution)/shard_map/ppermute | solution.py:412
  49.3 6.9 %collective-permute-done.10.arrivals_and_outs_2_ = f32[64,512]{1,0:T(8,128)S(1)} collective-permute-done((f32[64,512]{1,0:T(8,128)S(1)}, f32[64,512]{1,0:T(8,128)S(1)}, u32[]{:S(2)}, u32[]{:S(2)}) %collective-permute-start.10) | collective-permute-done | bytes 131104 | tf_op jit(solution)/shard_map/ppermute | solution.py:412
  56.5 0.7 %collective-permute-start.11 = (f32[64,512]{1,0:T(8,128)S(1)}, f32[64,512]{1,0:T(8,128)S(1)}, u32[]{:S(2)}, u32[]{:S(2)}) collective-permute-start(f32[64,512]{1,0:T(8,128)S(1)} %get-tuple-element.40), channel_id=1, source_target_pairs={{0,4},{4,0},{8,12},{12,8},{16,20},{20,16},{24,28},{28,24},{1,5},{5... | collective-permute-start | bytes 393224 | tf_op jit(solution)/shard_map/ppermute | solution.py:419
  57.2 0.6 collective-permute-done.5.arrivals_and_outs_2_
  58.2 0.9 %collective-permute-start.6 = (f32[64,512]{1,0:T(8,128)S(1)}, f32[64,512]{1,0:T(8,128)S(1)}, u32[]{:S(2)}, u32[]{:S(2)}) collective-permute-start(f32[64,512]{1,0:T(8,128)S(1)} %get-tuple-element.32), channel_id=1, source_target_pairs={{0,4},{4,0},{8,12},{12,8},{16,20},{20,16},{24,28},{28,24},{1,5},{5... | collective-permute-start | bytes 393224 | tf_op jit(solution)/shard_map/ppermute | solution.py:419
  59.4 0.4 shard_map.108
  59.8 1.8 %collective-permute-done.11.ahead = f32[64,512]{1,0:T(8,128)S(1)} collective-permute-done((f32[64,512]{1,0:T(8,128)S(1)}, f32[64,512]{1,0:T(8,128)S(1)}, u32[]{:S(2)}, u32[]{:S(2)}) %collective-permute-start.11) | collective-permute-done | bytes 131104 | tf_op jit(solution)/shard_map/ppermute | solution.py:419
  62.0 1.2 %collective-permute-done.6.ahead = f32[64,512]{1,0:T(8,128)S(1)} collective-permute-done((f32[64,512]{1,0:T(8,128)S(1)}, f32[64,512]{1,0:T(8,128)S(1)}, u32[]{:S(2)}, u32[]{:S(2)}) %collective-permute-start.6) | collective-permute-done | bytes 131104 | tf_op jit(solution)/shard_map/ppermute | solution.py:419
  63.2 1.2 %shard_map.109 = (f32[1,256,512]{2,1,0:T(8,128)}, f32[1,256]{1,0:T(1,128)}) custom-call(f32[64,512]{1,0:T(8,128)S(1)} %collective-permute-done.6.ahead, f32[64,512]{1,0:T(8,128)S(1)} %copy-done.5, f32[1,256,512]{2,1,0:T(8,128)S(1)} %copy-done, bf16[512,512]{1,0:T(8,128)(2,1)S(1)} %get-tuple-element.33.own_high, ...), custom_call_target="tpu_custom_call" | custom-call | tf_op jit(solution)/shard_map/pallas_call | solution.py:376
  (27 shorter events, 3.2 us)
Async XLA Ops:
  0.6 34.6 %copy-start.1 = (f32[1,512,512]{2,1,0:T(8,128)S(1)}, f32[1,512,512]{2,1,0:T(8,128)}, u32[]{:S(2)}) copy-start(f32[1,512,512]{2,1,0:T(8,128)} %own.3) | copy-start | bytes 3145732
  0.6 17.1 %collective-permute-start.1 = (f32[1,512,512]{2,1,0:T(8,128)}, f32[1,512,512]{2,1,0:T(8,128)}, u32[]{:S(2)}, u32[]{:S(2)}) collective-permute-start(f32[1,512,512]{2,1,0:T(8,128)} %own.3), channel_id=1, source_target_pairs={{0,4},{2,6},{4,0},{6,2},{8,12},{10,14},{12,8},{14,10},{16,20},{18,... | collective-permute-start | bytes 3145736 | tf_op jit(solution)/shard_map/ppermute | solution.py:395
  17.8 17.5 %collective-permute-start.2 = (f32[1,512,512]{2,1,0:T(8,128)}, f32[1,512,512]{2,1,0:T(8,128)}, u32[]{:S(2)}, u32[]{:S(2)}) collective-permute-start(f32[1,512,512]{2,1,0:T(8,128)} %collective-permute-done.1.got), channel_id=1, source_target_pairs={{0,1},{2,3},{4,5},{6,7},{8,9},{10,11},{12,13},{14,15},{16,17},{18,... | collective-permute-start | bytes 3145736 | tf_op jit(solution)/shard_map/ppermute | solution.py:402
  33.2 5.3 %copy-start.3 = (f32[64,512]{1,0:T(8,128)S(1)}, f32[64,512]{1,0:T(8,128)}, u32[]{:S(2)}) copy-start(f32[64,512]{1,0:T(8,128)} %get-tuple-element.35.kept.jump) | copy-start | bytes 393220
  33.2 5.2 %collective-permute-start.7 = (f32[64,512]{1,0:T(8,128)}, f32[64,512]{1,0:T(8,128)S(1)}, u32[]{:S(2)}, u32[]{:S(2)}) collective-permute-start(f32[64,512]{1,0:T(8,128)} %get-tuple-element.36.jump), channel_id=1, source_target_pairs={{0,4},{4,0},{8,12},{12,8},{16,20},{20,16},{24,28},{28,24},{1,5},{5... | collective-permute-start | bytes 393224 | tf_op jit(solution)/shard_map/ppermute | solution.py:401
  33.8 6.1 %copy-start.2 = (f32[64,512]{1,0:T(8,128)S(1)}, f32[64,512]{1,0:T(8,128)}, u32[]{:S(2)}) copy-start(f32[64,512]{1,0:T(8,128)} %get-tuple-element.24.kept.jump) | copy-start | bytes 393220
  33.8 6.1 %collective-permute-start = (f32[64,512]{1,0:T(8,128)}, f32[64,512]{1,0:T(8,128)S(1)}, u32[]{:S(2)}, u32[]{:S(2)}) collective-permute-start(f32[64,512]{1,0:T(8,128)} %get-tuple-element.25.jump), channel_id=1, source_target_pairs={{0,4},{4,0},{8,12},{12,8},{16,20},{20,16},{24,28},{28,24},{1,5},{5... | collective-permute-start | bytes 393224 | tf_op jit(solution)/shard_map/ppermute | solution.py:401
  38.7 5.2 %collective-permute-start.8 = (f32[64,512]{1,0:T(8,128)S(1)}, f32[64,512]{1,0:T(8,128)S(1)}, u32[]{:S(2)}, u32[]{:S(2)}) collective-permute-start(f32[64,512]{1,0:T(8,128)S(1)} %shard_map.102.joined), channel_id=1, source_target_pairs={{0,8},{4,12},{1,9},{5,13},{2,10},{6,14},{3,11},{7,15}} | collective-permute-start | bytes 393224 | tf_op jit(solution)/shard_map/ppermute | solution.py:412
  40.1 4.8 %collective-permute-start.3 = (f32[64,512]{1,0:T(8,128)S(1)}, f32[64,512]{1,0:T(8,128)S(1)}, u32[]{:S(2)}, u32[]{:S(2)}) collective-permute-start(f32[64,512]{1,0:T(8,128)S(1)} %shard_map.98.joined), channel_id=1, source_target_pairs={{0,8},{4,12},{1,9},{5,13},{2,10},{6,14},{3,11},{7,15}} | collective-permute-start | bytes 393224 | tf_op jit(solution)/shard_map/ppermute | solution.py:412
  44.2 1.7 %collective-permute-start.9 = (f32[64,512]{1,0:T(8,128)S(1)}, f32[64,512]{1,0:T(8,128)S(1)}, u32[]{:S(2)}, u32[]{:S(2)}) collective-permute-start(f32[64,512]{1,0:T(8,128)S(1)} %shard_map.103), channel_id=1, source_target_pairs={{8,16},{12,20},{9,17},{13,21},{10,18},{14,22},{11,19},{15,23}} | collective-permute-start | bytes 393224 | tf_op jit(solution)/shard_map/ppermute | solution.py:412
  45.2 2.4 %collective-permute-start.4 = (f32[64,512]{1,0:T(8,128)S(1)}, f32[64,512]{1,0:T(8,128)S(1)}, u32[]{:S(2)}, u32[]{:S(2)}) collective-permute-start(f32[64,512]{1,0:T(8,128)S(1)} %shard_map.99), channel_id=1, source_target_pairs={{8,16},{12,20},{9,17},{13,21},{10,18},{14,22},{11,19},{15,23}} | collective-permute-start | bytes 393224 | tf_op jit(solution)/shard_map/ppermute | solution.py:412
  46.2 12.8 %copy-start = (f32[1,256,512]{2,1,0:T(8,128)S(1)}, f32[1,256,512]{2,1,0:T(8,128)}, u32[]{:S(2)}) copy-start(f32[1,256,512]{2,1,0:T(8,128)} %start.9) | copy-start | bytes 1572868
  46.2 10.0 %collective-permute-start.10 = (f32[64,512]{1,0:T(8,128)S(1)}, f32[64,512]{1,0:T(8,128)S(1)}, u32[]{:S(2)}, u32[]{:S(2)}) collective-permute-start(f32[64,512]{1,0:T(8,128)S(1)} %shard_map.104), channel_id=1, source_target_pairs={{16,24},{20,28},{17,25},{21,29},{18,26},{22,30},{19,27},{23,31}} | collective-permute-start | bytes 393224 | tf_op jit(solution)/shard_map/ppermute | solution.py:412
  48.0 9.9 %collective-permute-start.5 = (f32[64,512]{1,0:T(8,128)S(1)}, f32[64,512]{1,0:T(8,128)S(1)}, u32[]{:S(2)}, u32[]{:S(2)}) collective-permute-start(f32[64,512]{1,0:T(8,128)S(1)} %shard_map.100), channel_id=1, source_target_pairs={{16,24},{20,28},{17,25},{21,29},{18,26},{22,30},{19,27},{23,31}} | collective-permute-start | bytes 393224 | tf_op jit(solution)/shard_map/ppermute | solution.py:412
  56.5 5.0 %collective-permute-start.11 = (f32[64,512]{1,0:T(8,128)S(1)}, f32[64,512]{1,0:T(8,128)S(1)}, u32[]{:S(2)}, u32[]{:S(2)}) collective-permute-start(f32[64,512]{1,0:T(8,128)S(1)} %get-tuple-element.40), channel_id=1, source_target_pairs={{0,4},{4,0},{8,12},{12,8},{16,20},{20,16},{24,28},{28,24},{1,5},{5... | collective-permute-start | bytes 393224 | tf_op jit(solution)/shard_map/ppermute | solution.py:419
  58.1 3.4 %copy-start.4 = (f32[64,512]{1,0:T(8,128)S(1)}, f32[64,512]{1,0:T(8,128)}, u32[]{:S(2)}) copy-start(f32[64,512]{1,0:T(8,128)} %get-tuple-element.36.jump) | copy-start | bytes 393220
  58.2 5.0 %collective-permute-start.6 = (f32[64,512]{1,0:T(8,128)S(1)}, f32[64,512]{1,0:T(8,128)S(1)}, u32[]{:S(2)}, u32[]{:S(2)}) collective-permute-start(f32[64,512]{1,0:T(8,128)S(1)} %get-tuple-element.32), channel_id=1, source_target_pairs={{0,4},{4,0},{8,12},{12,8},{16,20},{20,16},{24,28},{28,24},{1,5},{5... | collective-permute-start | bytes 393224 | tf_op jit(solution)/shard_map/ppermute | solution.py:419
  59.4 3.8 %copy-start.5 = (f32[64,512]{1,0:T(8,128)S(1)}, f32[64,512]{1,0:T(8,128)}, u32[]{:S(2)}) copy-start(f32[64,512]{1,0:T(8,128)} %get-tuple-element.25.jump) | copy-start | bytes 393220

commit v4 on v3

--- a/solution.py
+++ b/solution.py
@@ -43,10 +43,6 @@
     return pl.BlockSpec(memory_space=pltpu.HBM)
 
 
-def place():
-    return lax.axis_index("layer"), lax.axis_index("dp") % 2
-
-
 def is_even():
     return lax.axis_index("layer") % 2 == 0
 
@@ -54,7 +50,10 @@
 def fine_kernel(
     lengths, start, gain, surrogate, w_qkv, w_out, w_up, w_down, *outs_and_scratch
 ):
-    *pieces, begun, scale, limits, w_in, w_back, varying, state, act, qkv, bias, sems = outs_and_scratch
+    (
+        *pieces, own_high, own_low, begun, scale, limits, w_in, w_back, varying, through,
+        state, act, qkv, bias, sems,
+    ) = outs_and_scratch
     tokens, width = state.shape
     hidden = w_back.shape[0] - width
     moves = (
@@ -140,6 +139,9 @@
             act[:, width + n : width + n + chunk] = gelu.astype(BF16)
 
         if first:
+            copies[7].wait()
+            own_high[...], own_low[...] = halves_of(0.3 * varying[...])
+            through[...] = 0.9 * begun[...] + dot_split(begun[...], own_high[...], own_low[...])
             copies[5].wait()
             copies[6].wait()
 
@@ -151,12 +153,9 @@
     def _(_):
         substep(False)
 
-    copies[7].wait()
-    layer, _ = place()
+    layer = lax.axis_index("layer")
     share = jnp.where(layer == 0, 0.0, 1.0).astype(F32)
-    high, low_part = halves_of(0.3 * varying[...])
-    through = 0.9 * begun[...] + dot_split(begun[...], high, low_part)
-    state[...] = state[...] - share * through
+    state[...] = state[...] - share * through[...]
     mine = layer % 2
     half = pieces[0].shape[0]
     for at in range(len(pieces) // 2):
@@ -168,11 +167,12 @@
     tokens, width = start.shape[1:]
     hidden = w_up.shape[2]
     half = jax.ShapeDtypeStruct((tokens // (2 * chunks), width), F32)
+    square = jax.ShapeDtypeStruct((width, width), BF16)
     return pl.pallas_call(
         fine_kernel,
         in_specs=[in_place()] * 8,
-        out_specs=[in_vmem()] * (2 * chunks),
-        out_shape=[half] * (2 * chunks),
+        out_specs=[in_vmem()] * (2 * chunks + 2),
+        out_shape=[half] * (2 * chunks) + [square] * 2,
         scratch_shapes=[
             pltpu.VMEM((tokens, width), F32),
             pltpu.VMEM(gain.shape, F32),
@@ -180,6 +180,7 @@
             pltpu.VMEM((width, 3 * width + hidden), BF16),
             pltpu.VMEM((width + hidden, width), BF16),
             pltpu.VMEM((width, width), F32),
+            pltpu.VMEM((tokens, width), F32),
             pltpu.VMEM((tokens, width), F32),
             pltpu.VMEM((tokens, width + hidden), BF16),
             pltpu.VMEM((tokens, 3 * width), BF16),
@@ -191,98 +192,82 @@
             transcendentals=FINE * tokens * hidden,
             bytes_accessed=2 * width * (4 * width + 2 * hidden),
         ),
-        compiler_params=params(62),
-    )(lengths, start, gain, surrogate, w_qkv, w_out, w_up, w_down)
-
-
-def partner_map(got, passed, other):
+        compiler_params=params(32),
+    )(*[pltpu.with_memory_space_constraint(a, pltpu.HBM) for a in (lengths, start, gain, surrogate, w_qkv, w_out, w_up, w_down)])
+
+
+def other_kernel(got, passed, high, low):
+    part = got.shape[0]
     core = lax.axis_index("dp") % 2
-
-    @pl.when(core == 0)
-    def _():
-        other[...] = 0.3 * got[0]
-
-    @pl.when(core != 0)
-    def _():
-        other[...] = 0.3 * passed[0]
-
-
-def odd_kernel(own, got, passed, odd_high, odd_low, other):
-    even = is_even()
-
-    @pl.when(even)
-    def _():
-        partner_map(got, passed, other)
-
-    @pl.when(jnp.logical_not(even))
-    def _():
-        other[...] = 0.3 * own[0]
-
-    odd_high[...], odd_low[...] = halves_of(other[...])
-
-
-def odd_map(own, got, passed):
-    width = own.shape[1]
-    square = jax.ShapeDtypeStruct((width, width), BF16)
-    return pl.pallas_call(
-        odd_kernel,
-        in_specs=[in_vmem()] * 3,
+    for source, where in ((got, core), (passed, 1 - core)):
+        rows = pl.ds(pl.multiple_of(where * part, part), part)
+        high[rows, :], low[rows, :] = halves_of(0.3 * source[...])
+
+
+def other_map(got, passed):
+    part, width = got.shape
+    square = jax.ShapeDtypeStruct((2 * part, width), BF16)
+    return pl.pallas_call(
+        other_kernel,
+        in_specs=[in_vmem()] * 2,
         out_specs=[in_vmem()] * 2,
         out_shape=[square] * 2,
-        scratch_shapes=[pltpu.VMEM((width, width), F32)],
-        compiler_params=params(8),
-    )(own, got, passed)
-
-
-def maps_kernel(
-    own, got, passed, odd_high, odd_low, own_high, own_low, even_high, even_low, both_high, both_low, other
-):
+        compiler_params=params(6),
+    )(got, passed)
+
+
+def both_kernel(own_high, own_low, other_high, other_low, both_high, both_low):
+    def product(first_high, first_low, second_high, second_low):
+        a_high, a_low = first_high[...], first_low[...]
+        b_high, b_low = second_high[...], second_low[...]
+        total = (a_high.astype(F32) + b_high.astype(F32)) + (a_low.astype(F32) + b_low.astype(F32))
+        dot = functools.partial(jnp.dot, preferred_element_type=F32)
+        value = 0.9 * total + (dot(a_high, b_high) + (dot(a_low, b_high) + dot(a_high, b_low)))
+        both_high[...], both_low[...] = halves_of(value)
+
     even = is_even()
 
     @pl.when(even)
     def _():
-        other[...] = 0.3 * own[0]
+        product(own_high, own_low, other_high, other_low)
 
     @pl.when(jnp.logical_not(even))
     def _():
-        partner_map(got, passed, other)
-
-    own_high[...], own_low[...] = halves_of(0.3 * own[0])
-    first = other[...]
-    even_high[...], even_low[...] = halves_of(first)
-    second = odd_high[...].astype(F32) + odd_low[...].astype(F32)
-    product = 0.9 * (first + second) + dot_split(first, odd_high[...], odd_low[...])
-    both_high[...], both_low[...] = halves_of(product)
-
-
-def maps(own, got, passed, odd):
-    width = own.shape[1]
-    square = jax.ShapeDtypeStruct((width, width), BF16)
-    return pl.pallas_call(
-        maps_kernel,
-        in_specs=[in_vmem()] * 5,
-        out_specs=[in_vmem()] * 6,
-        out_shape=[square] * 6,
-        scratch_shapes=[pltpu.VMEM((width, width), F32)],
-        compiler_params=params(14),
-    )(own, got, passed, *odd)
-
-
-def join_kernel(kept, received, odd_high, odd_low, out):
+        product(other_high, other_low, own_high, own_low)
+
+
+def both_map(own, other):
+    return pl.pallas_call(
+        both_kernel,
+        in_specs=[in_vmem()] * 4,
+        out_specs=[in_vmem()] * 2,
+        out_shape=[jax.ShapeDtypeStruct(part.shape, BF16) for part in own],
+        compiler_params=params(10),
+    )(*own, *other)
+
+
+def join_kernel(kept, received, own_high, own_low, other_high, other_low, out):
     even = is_even()
-    first = jnp.where(even, kept[...], received[...])
-    second = jnp.where(even, received[...], kept[...])
-    out[...] = second + (0.9 * first + dot_split(first, odd_high[...], odd_low[...]))
-
-
-def join(kept, received, odd):
+
+    @pl.when(even)
+    def _():
+        first = kept[...]
+        out[...] = received[...] + (0.9 * first + dot_split(first, other_high[...], other_low[...]))
+
+    @pl.when(jnp.logical_not(even))
+    def _():
+        first = received[...]
+        out[...] = kept[...] + (0.9 * first + dot_split(first, own_high[...], own_low[...]))
+
+
+def join(kept, received, own, other):
     return pl.pallas_call(
         join_kernel,
-        in_specs=[in_vmem()] * 4,
+        in_specs=[in_vmem()] * 6,
         out_specs=in_vmem(),
         out_shape=jax.ShapeDtypeStruct(kept.shape, F32),
         compiler_params=params(8),
-    )(kept, received, *odd)
+    )(kept, received, *own, *other)
 
 
 def hop_kernel(incoming, joined, both_high, both_low, out):
@@ -300,25 +285,33 @@
     )(incoming, joined, *both)
 
 
-def turn_kernel(kept, received, even_high, even_low, *arrivals_and_outs):
+def turn_kernel(
+    kept, received, own_high, own_low, other_high, other_low, *arrivals_and_outs
+):
     *arrivals, head, out = arrivals_and_outs
     state = functools.reduce(jnp.add, [arrival[...] for arrival in arrivals])
     even = is_even()
-    first = jnp.where(even, kept[...], received[...])
-    after = first + (0.9 * state + dot_split(state, even_high[...], even_low[...]))
-    head[...] = jnp.where(even, state, after)
-    out[...] = jnp.where(even, after, state)
-
-
-def turn(kept, received, even, arrivals):
+
+    @pl.when(even)
+    def _():
+        head[...] = state
+        out[...] = kept[...] + (0.9 * state + dot_split(state, own_high[...], own_low[...]))
+
+    @pl.when(jnp.logical_not(even))
+    def _():
+        out[...] = state
+        head[...] = received[...] + (0.9 * state + dot_split(state, other_high[...], other_low[...]))
+
+
+def turn(kept, received, own, other, arrivals):
     shape = jax.ShapeDtypeStruct(kept.shape, F32)
     return pl.pallas_call(
         turn_kernel,
-        in_specs=[in_vmem()] * (4 + len(arrivals)),
+        in_specs=[in_vmem()] * (6 + len(arrivals)),
         out_specs=[in_vmem()] * 2,
         out_shape=[shape, shape],
         compiler_params=params(8),
-    )(kept, received, *even, *arrivals)
+    )(kept, received, *own, *other, *arrivals)
 
 
 def part_of(row, ahead, jump, start, own_high, own_low):
@@ -389,21 +382,24 @@
     layers = lax.axis_size("layer")
     batches = lax.axis_size("dp")
     partners = [(i, i ^ 1) for i in range(layers)]
-    ports = [
-        (i * batches + j, (i ^ 1) * batches + j) for i in range(layers) for j in range(0, batches, 2)
-    ]
-    got = lax.ppermute(surrogate, ("layer", "dp"), ports)
-    pieces = fine_jump(CHUNKS, lengths, old_heads, norm_gain, surrogate, w_qkv, w_out, w_up, w_down)
+    neighbours = [(i, i ^ 1) for i in range(batches)]
+    half = surrogate.shape[1] // 2
+    core = lax.axis_index("dp") % 2
+    mine = lax.dynamic_slice_in_dim(surrogate[0], core * half, half, 0)
+    got = lax.ppermute(mine, "layer", partners)
+    *pieces, own_high, own_low = fine_jump(
+        CHUNKS, lengths, old_heads, norm_gain, surrogate, w_qkv, w_out, w_up, w_down
+    )
+    own = own_high, own_low
     kept, sent = pieces[::2], pieces[1::2]
     spans = range(CHUNKS)
     received = []
     for c in spans:
         received.append(lax.ppermute(sent[c], "layer", partners))
-    passed = lax.ppermute(got, "dp", [(i, i + 1) for i in range(0, batches - 1, 2)])
-    odd = odd_map(surrogate, got, passed)
-    split = maps(surrogate, got, passed, odd)
-    own, even, both = split[0:2], split[2:4], split[4:6]
-    joined = [join(kept[c], received[c], odd) for c in spans]
+    passed = lax.ppermute(got, "dp", neighbours)
+    other = other_map(got, passed)
+    both = both_map(own, other)
+    joined = [join(kept[c], received[c], own, other) for c in spans]
     carried = joined
     arrivals = [[] for c in spans]
     for at in range(0, layers - 2, 2):
@@ -414,7 +410,7 @@
             carried = [hop(arrivals[c][-1], joined[c], both) for c in spans]
     heads, returned = [], []
     for c in spans:
-        head, out = turn(kept[c], received[c], even, arrivals[c])
+        head, out = turn(kept[c], received[c], own, other, arrivals[c])
         heads.append(head)
         returned.append(lax.ppermute(out, "layer", partners))
     done = []

time: 65 us -> 62.5 us (0.962)
  waiting for transfers between devices: 26.9 us -> 32.3 us
  starting transfers between devices: 13.9 us -> 9.31 us
  Pallas kernels: 22.7 us -> 18.6 us
  local copies, waits for them, and re-layouts: 0.03 us -> 1.09 us
    ppermute x2, starting transfers between devices: 4.83 us -> 0.6 us  [the longest x1 0.6 us: shards(): got = lax.ppermute(mine, 'layer', partners)]
    ppermute x2, waiting for transfers between devices: 1.78 us -> 5.45 us  [shards(): received.append(lax.ppermute(sent[c], 'layer', partners))]
    pallas_call x6, Pallas kernels: 6.1 us -> 2.7 us  [the longest x1 1.23 us: both_map(): pl.pallas_call(both_kernel, in_specs=[in_vmem()] * 4, out_specs=[in_vmem(...]
    ppermute x6, waiting for transfers between devices: 7.56 us -> 9.95 us  [shards(): arrivals[c].append(lax.ppermute(carried[c], 'layer', route))]
    ppermute x2, waiting for transfers between devices: 14.6 us -> 13.1 us  [the longest x1 13.1 us: shards(): got = lax.ppermute(mine, 'layer', partners)]
    dynamic_slice x0 -> x1, local copies, waits for them, and re-layouts: none -> 1.08 us  [shards(): mine = lax.dynamic_slice_in_dim(surrogate[0], core * half, half, 0)]
    ppermute x2, waiting for transfers between devices: 2.98 us -> 3.78 us  [shards(): returned.append(lax.ppermute(out, 'layer', partners))]
    pallas_call x1, Pallas kernels: 13.1 us -> 12.4 us  [fine_jump(): pl.pallas_call(fine_kernel, in_specs=[in_place()] * 8, out_specs=[in_vmem...]
  transfers between devices with their start and end apart: 12 -> 12, of which waited for: 7 -> 7; matrix products, arithmetic and copies ran while one was open for 0% -> 0% of each run, Pallas kernels for 33% -> 28%
where the time goes in v4:
time: 62.5 us; the launch traced here: 62.2 us
  waiting for transfers between devices  32.3 us (52%)
  Pallas kernels  18.6 us (30%)
  starting transfers between devices  9.31 us (15%)
  local copies, waits for them, and re-layouts  1.09 us (2%)
  between operations  0.85 us (1%)
    ppermute x1, waiting for transfers between devices, shards(): got = lax.ppermute(mine, 'layer', partners)  13.1 us
    pallas_call x1, Pallas kernels, fine_jump(): pl.pallas_call(fine_kernel, in_specs=[in_place()] * 8, out_specs=[in_vmem...  12.4 us
    ppermute x6, waiting for transfers between devices, shards(): arrivals[c].append(lax.ppermute(carried[c], 'layer', route))  9.95 us
    ppermute x2, waiting for transfers between devices, shards(): received.append(lax.ppermute(sent[c], 'layer', partners))  5.45 us
    ppermute x6, starting transfers between devices, shards(): arrivals[c].append(lax.ppermute(carried[c], 'layer', route))  5.39 us
    ppermute x2, waiting for transfers between devices, shards(): returned.append(lax.ppermute(out, 'layer', partners))  3.78 us
    ppermute x2, starting transfers between devices, shards(): received.append(lax.ppermute(sent[c], 'layer', partners))  2.09 us
  transfers between devices with their start and end apart: 12, of which 7 were waited for; matrix products, arithmetic and copies ran while one was open for 0% of the time, Pallas kernels for 28%

profile of v4, /device:TPU:26, one launch (start us, length us, event | category | flops | bytes accessed | tf_op | source)
XLA Modules:
  0.0 62.2 jit_solution(16999166165679661924)
XLA Ops:
  0.6 1.1 %dynamic-slice_bitcast_fusion = f32[256,512]{1,0:T(8,128)S(1)} fusion(f32[1,512,512]{2,1,0:T(8,128)} %surrogate.1, s32[]{:T(128)S(6)} %select_n.11), kind=kLoop, calls=%fused_computation | loop fusion | bytes 1048580 | tf_op jit(solution)/shard_map/dynamic_slice | solution.py:388
  1.7 0.6 collective-permute-start.1
  2.3 13.1 %collective-permute-done.1.got = f32[256,512]{1,0:T(8,128)S(1)} collective-permute-done((f32[256,512]{1,0:T(8,128)S(1)}, f32[256,512]{1,0:T(8,128)S(1)}, u32[]{:S(2)}, u32[]{:S(2)}) %collective-permute-start.1) | collective-permute-done | bytes 524320 | tf_op jit(solution)/shard_map/ppermute | solution.py:389
  15.5 12.4 %shard_map.95 = (f32[64,512]{1,0:T(8,128)S(1)}, f32[64,512]{1,0:T(8,128)S(1)}, f32[64,512]{1,0:T(8,128)S(1)}, f32[64,512]{1,0:T(8,128)S(1)}, bf16[512,512]{1,0:T(8,128)(2,1)S(1)}, /*index=5*/bf16[512,512]{1,0:T(8,128)(2,1)S(1)}) custom-call(s32[2]{0:T(128)} %lengths.1, f32[1,256,512]{2,1,0:T(8,128)} %start.9, f32[1,512]{1,0:T(1,128)} %gain.1, ...), custom_call_target="tpu_custom_call" | custom-call | flops 6442450944 | bytes 6291456 | tf_op jit(solution)/shard_map/pallas_call | solution.py:171
  27.9 0.6 collective-permute-start.7
  28.5 1.5 %collective-permute-start = (f32[64,512]{1,0:T(8,128)S(1)}, f32[64,512]{1,0:T(8,128)S(1)}, u32[]{:S(2)}, u32[]{:S(2)}) collective-permute-start(f32[64,512]{1,0:T(8,128)S(1)} %get-tuple-element.23.jump), channel_id=1, source_target_pairs={{0,4},{4,0},{8,12},{12,8},{16,20},{20,16},{24,28},{28,24},{1,5},{5... | collective-permute-start | bytes 393224 | tf_op jit(solution)/shard_map/ppermute | solution.py:398
  30.3 4.1 %collective-permute-done.7.received = f32[64,512]{1,0:T(8,128)S(1)} collective-permute-done((f32[64,512]{1,0:T(8,128)S(1)}, f32[64,512]{1,0:T(8,128)S(1)}, u32[]{:S(2)}, u32[]{:S(2)}) %collective-permute-start.7) | collective-permute-done | bytes 131104 | tf_op jit(solution)/shard_map/ppermute | solution.py:398
  34.6 0.7 %collective-permute-start.8 = (f32[64,512]{1,0:T(8,128)S(1)}, f32[64,512]{1,0:T(8,128)S(1)}, u32[]{:S(2)}, u32[]{:S(2)}) collective-permute-start(f32[64,512]{1,0:T(8,128)S(1)} %shard_map.102.joined), channel_id=1, source_target_pairs={{0,8},{4,12},{1,9},{5,13},{2,10},{6,14},{3,11},{7,15}} | collective-permute-start | bytes 393224 | tf_op jit(solution)/shard_map/ppermute | solution.py:408
  35.3 1.4 %collective-permute-done.received = f32[64,512]{1,0:T(8,128)S(1)} collective-permute-done((f32[64,512]{1,0:T(8,128)S(1)}, f32[64,512]{1,0:T(8,128)S(1)}, u32[]{:S(2)}, u32[]{:S(2)}) %collective-permute-start) | collective-permute-done | bytes 131104 | tf_op jit(solution)/shard_map/ppermute | solution.py:398
  37.0 0.7 %collective-permute-start.3 = (f32[64,512]{1,0:T(8,128)S(1)}, f32[64,512]{1,0:T(8,128)S(1)}, u32[]{:S(2)}, u32[]{:S(2)}) collective-permute-start(f32[64,512]{1,0:T(8,128)S(1)} %shard_map.97.joined), channel_id=1, source_target_pairs={{0,8},{4,12},{1,9},{5,13},{2,10},{6,14},{3,11},{7,15}} | collective-permute-start | bytes 393224 | tf_op jit(solution)/shard_map/ppermute | solution.py:408
  37.7 1.2 %shard_map.98 = (bf16[512,512]{1,0:T(8,128)(2,1)S(1)}, bf16[512,512]{1,0:T(8,128)(2,1)S(1)}) custom-call(bf16[512,512]{1,0:T(8,128)(2,1)S(1)} %get-tuple-element.24.own_high, bf16[512,512]{1,0:T(8,128)(2,1)S(1)} %get-tuple-element.25.own_low, bf16[512,512]{1,0:T(8,128)(2,1)S(1)} %get-tuple-element.26.other_high, bf16[512,512]{1,0:T(8,128)(2,1)S(1)} %get-tuple-element.27.other_low), custom_call_target="tpu_custom_call" | custom-call | tf_op jit(solution)/shard_map/pallas_call | solution.py:240
  39.2 0.7 %collective-permute-start.9 = (f32[64,512]{1,0:T(8,128)S(1)}, f32[64,512]{1,0:T(8,128)S(1)}, u32[]{:S(2)}, u32[]{:S(2)}) collective-permute-start(f32[64,512]{1,0:T(8,128)S(1)} %shard_map.103), channel_id=1, source_target_pairs={{8,16},{12,20},{9,17},{13,21},{10,18},{14,22},{11,19},{15,23}} | collective-permute-start | bytes 393224 | tf_op jit(solution)/shard_map/ppermute | solution.py:408
  40.2 0.7 %collective-permute-start.4 = (f32[64,512]{1,0:T(8,128)S(1)}, f32[64,512]{1,0:T(8,128)S(1)}, u32[]{:S(2)}, u32[]{:S(2)}) collective-permute-start(f32[64,512]{1,0:T(8,128)S(1)} %shard_map.99), channel_id=1, source_target_pairs={{8,16},{12,20},{9,17},{13,21},{10,18},{14,22},{11,19},{15,23}} | collective-permute-start | bytes 393224 | tf_op jit(solution)/shard_map/ppermute | solution.py:408
  41.2 1.3 %collective-permute-start.10 = (f32[64,512]{1,0:T(8,128)S(1)}, f32[64,512]{1,0:T(8,128)S(1)}, u32[]{:S(2)}, u32[]{:S(2)}) collective-permute-start(f32[64,512]{1,0:T(8,128)S(1)} %shard_map.104), channel_id=1, source_target_pairs={{16,24},{20,28},{17,25},{21,29},{18,26},{22,30},{19,27},{23,31}} | collective-permute-start | bytes 393224 | tf_op jit(solution)/shard_map/ppermute | solution.py:408
  42.8 1.4 %collective-permute-start.5 = (f32[64,512]{1,0:T(8,128)S(1)}, f32[64,512]{1,0:T(8,128)S(1)}, u32[]{:S(2)}, u32[]{:S(2)}) collective-permute-start(f32[64,512]{1,0:T(8,128)S(1)} %shard_map.100), channel_id=1, source_target_pairs={{16,24},{20,28},{17,25},{21,29},{18,26},{22,30},{19,27},{23,31}} | collective-permute-start | bytes 393224 | tf_op jit(solution)/shard_map/ppermute | solution.py:408
  44.2 8.6 %collective-permute-done.10.arrivals_and_outs_2_ = f32[64,512]{1,0:T(8,128)S(1)} collective-permute-done((f32[64,512]{1,0:T(8,128)S(1)}, f32[64,512]{1,0:T(8,128)S(1)}, u32[]{:S(2)}, u32[]{:S(2)}) %collective-permute-start.10) | collective-permute-done | bytes 131104 | tf_op jit(solution)/shard_map/ppermute | solution.py:408
  53.2 0.6 collective-permute-start.11
  53.8 1.3 %collective-permute-done.5.arrivals_and_outs_2_ = f32[64,512]{1,0:T(8,128)S(1)} collective-permute-done((f32[64,512]{1,0:T(8,128)S(1)}, f32[64,512]{1,0:T(8,128)S(1)}, u32[]{:S(2)}, u32[]{:S(2)}) %collective-permute-start.5) | collective-permute-done | bytes 131104 | tf_op jit(solution)/shard_map/ppermute | solution.py:408
  55.4 0.6 collective-permute-start.6
  56.0 0.4 shard_map.108
  56.4 0.4 shard_map.106
  56.8 2.4 %collective-permute-done.11.ahead = f32[64,512]{1,0:T(8,128)S(1)} collective-permute-done((f32[64,512]{1,0:T(8,128)S(1)}, f32[64,512]{1,0:T(8,128)S(1)}, u32[]{:S(2)}, u32[]{:S(2)}) %collective-permute-start.11) | collective-permute-done | bytes 131104 | tf_op jit(solution)/shard_map/ppermute | solution.py:415
  59.6 1.4 %collective-permute-done.6.ahead = f32[64,512]{1,0:T(8,128)S(1)} collective-permute-done((f32[64,512]{1,0:T(8,128)S(1)}, f32[64,512]{1,0:T(8,128)S(1)}, u32[]{:S(2)}, u32[]{:S(2)}) %collective-permute-start.6) | collective-permute-done | bytes 131104 | tf_op jit(solution)/shard_map/ppermute | solution.py:415
  61.0 1.2 %shard_map.109 = (f32[1,256,512]{2,1,0:T(8,128)}, f32[1,256]{1,0:T(1,128)}) custom-call(f32[64,512]{1,0:T(8,128)S(1)} %collective-permute-done.6.ahead, f32[64,512]{1,0:T(8,128)S(1)} %get-tuple-element.23.jump, f32[1,256,512]{2,1,0:T(8,128)S(1)} %copy-done, bf16[512,512]{1,0:T(8,128)(2,1)S(1)} %get-tuple-element.24.own_high, ...), custom_call_target="tpu_custom_call" | custom-call | tf_op jit(solution)/shard_map/pallas_call | solution.py:369
  (18 shorter events, 3.0 us)
Async XLA Ops:
  1.7 13.7 %collective-permute-start.1 = (f32[256,512]{1,0:T(8,128)S(1)}, f32[256,512]{1,0:T(8,128)S(1)}, u32[]{:S(2)}, u32[]{:S(2)}) collective-permute-start(f32[256,512]{1,0:T(8,128)S(1)} %dynamic-slice_bitcast_fusion), channel_id=1, source_target_pairs={{0,4},{4,0},{8,12},{12,8},{16,20},{20,16},{24,28},{28,24},{1,5},{5... | collective-permute-start | bytes 1572872 | tf_op jit(solution)/shard_map/ppermute | solution.py:389
  15.5 14.5 %collective-permute-start.2 = (f32[256,512]{1,0:T(8,128)S(1)}, f32[256,512]{1,0:T(8,128)S(1)}, u32[]{:S(2)}, u32[]{:S(2)}) collective-permute-start(f32[256,512]{1,0:T(8,128)S(1)} %collective-permute-done.1.got), channel_id=1, source_target_pairs={{0,1},{1,0},{2,3},{3,2},{4,5},{5,4},{6,7},{7,6},{8,9},{9,8},{10,11... | collective-permute-start | bytes 1572872 | tf_op jit(solution)/shard_map/ppermute | solution.py:399
  27.9 6.4 %collective-permute-start.7 = (f32[64,512]{1,0:T(8,128)S(1)}, f32[64,512]{1,0:T(8,128)S(1)}, u32[]{:S(2)}, u32[]{:S(2)}) collective-permute-start(f32[64,512]{1,0:T(8,128)S(1)} %get-tuple-element.32.jump), channel_id=1, source_target_pairs={{0,4},{4,0},{8,12},{12,8},{16,20},{20,16},{24,28},{28,24},{1,5},{5... | collective-permute-start | bytes 393224 | tf_op jit(solution)/shard_map/ppermute | solution.py:398
  28.5 8.2 %collective-permute-start = (f32[64,512]{1,0:T(8,128)S(1)}, f32[64,512]{1,0:T(8,128)S(1)}, u32[]{:S(2)}, u32[]{:S(2)}) collective-permute-start(f32[64,512]{1,0:T(8,128)S(1)} %get-tuple-element.23.jump), channel_id=1, source_target_pairs={{0,4},{4,0},{8,12},{12,8},{16,20},{20,16},{24,28},{28,24},{1,5},{5... | collective-permute-start | bytes 393224 | tf_op jit(solution)/shard_map/ppermute | solution.py:398
  34.6 4.3 %collective-permute-start.8 = (f32[64,512]{1,0:T(8,128)S(1)}, f32[64,512]{1,0:T(8,128)S(1)}, u32[]{:S(2)}, u32[]{:S(2)}) collective-permute-start(f32[64,512]{1,0:T(8,128)S(1)} %shard_map.102.joined), channel_id=1, source_target_pairs={{0,8},{4,12},{1,9},{5,13},{2,10},{6,14},{3,11},{7,15}} | collective-permute-start | bytes 393224 | tf_op jit(solution)/shard_map/ppermute | solution.py:408
  37.0 2.9 %collective-permute-start.3 = (f32[64,512]{1,0:T(8,128)S(1)}, f32[64,512]{1,0:T(8,128)S(1)}, u32[]{:S(2)}, u32[]{:S(2)}) collective-permute-start(f32[64,512]{1,0:T(8,128)S(1)} %shard_map.97.joined), channel_id=1, source_target_pairs={{0,8},{4,12},{1,9},{5,13},{2,10},{6,14},{3,11},{7,15}} | collective-permute-start | bytes 393224 | tf_op jit(solution)/shard_map/ppermute | solution.py:408
  39.2 1.7 %collective-permute-start.9 = (f32[64,512]{1,0:T(8,128)S(1)}, f32[64,512]{1,0:T(8,128)S(1)}, u32[]{:S(2)}, u32[]{:S(2)}) collective-permute-start(f32[64,512]{1,0:T(8,128)S(1)} %shard_map.103), channel_id=1, source_target_pairs={{8,16},{12,20},{9,17},{13,21},{10,18},{14,22},{11,19},{15,23}} | collective-permute-start | bytes 393224 | tf_op jit(solution)/shard_map/ppermute | solution.py:408
  40.2 2.3 %collective-permute-start.4 = (f32[64,512]{1,0:T(8,128)S(1)}, f32[64,512]{1,0:T(8,128)S(1)}, u32[]{:S(2)}, u32[]{:S(2)}) collective-permute-start(f32[64,512]{1,0:T(8,128)S(1)} %shard_map.99), channel_id=1, source_target_pairs={{8,16},{12,20},{9,17},{13,21},{10,18},{14,22},{11,19},{15,23}} | collective-permute-start | bytes 393224 | tf_op jit(solution)/shard_map/ppermute | solution.py:408
  41.2 11.7 %collective-permute-start.10 = (f32[64,512]{1,0:T(8,128)S(1)}, f32[64,512]{1,0:T(8,128)S(1)}, u32[]{:S(2)}, u32[]{:S(2)}) collective-permute-start(f32[64,512]{1,0:T(8,128)S(1)} %shard_map.104), channel_id=1, source_target_pairs={{16,24},{20,28},{17,25},{21,29},{18,26},{22,30},{19,27},{23,31}} | collective-permute-start | bytes 393224 | tf_op jit(solution)/shard_map/ppermute | solution.py:408
  42.8 13.3 %copy-start = (f32[1,256,512]{2,1,0:T(8,128)S(1)}, f32[1,256,512]{2,1,0:T(8,128)}, u32[]{:S(2)}) copy-start(f32[1,256,512]{2,1,0:T(8,128)} %start.9) | copy-start | bytes 1572868
  42.8 12.3 %collective-permute-start.5 = (f32[64,512]{1,0:T(8,128)S(1)}, f32[64,512]{1,0:T(8,128)S(1)}, u32[]{:S(2)}, u32[]{:S(2)}) collective-permute-start(f32[64,512]{1,0:T(8,128)S(1)} %shard_map.100), channel_id=1, source_target_pairs={{16,24},{20,28},{17,25},{21,29},{18,26},{22,30},{19,27},{23,31}} | collective-permute-start | bytes 393224 | tf_op jit(solution)/shard_map/ppermute | solution.py:408
  53.2 6.1 %collective-permute-start.11 = (f32[64,512]{1,0:T(8,128)S(1)}, f32[64,512]{1,0:T(8,128)S(1)}, u32[]{:S(2)}, u32[]{:S(2)}) collective-permute-start(f32[64,512]{1,0:T(8,128)S(1)} %get-tuple-element.36), channel_id=1, source_target_pairs={{0,4},{4,0},{8,12},{12,8},{16,20},{20,16},{24,28},{28,24},{1,5},{5... | collective-permute-start | bytes 393224 | tf_op jit(solution)/shard_map/ppermute | solution.py:415
  55.4 5.6 %collective-permute-start.6 = (f32[64,512]{1,0:T(8,128)S(1)}, f32[64,512]{1,0:T(8,128)S(1)}, u32[]{:S(2)}, u32[]{:S(2)}) collective-permute-start(f32[64,512]{1,0:T(8,128)S(1)} %get-tuple-element.30), channel_id=1, source_target_pairs={{0,4},{4,0},{8,12},{12,8},{16,20},{20,16},{24,28},{28,24},{1,5},{5... | collective-permute-start | bytes 393224 | tf_op jit(solution)/shard_map/ppermute | solution.py:415

commit v5 on v4

--- a/solution.py
+++ b/solution.py
@@ -319,9 +319,10 @@
     state = ahead[...]
     new = jump[...] + (0.9 * state + dot_split(state, own_high[...], own_low[...]))
     difference = state - start[0, pl.ds(pl.multiple_of(row * half, half), half), :]
-    total = lax.dot_general(
-        jnp.ones((8, width), F32), difference * difference, (((1,), (1,)), ((), ())),
-        precision=lax.Precision.HIGHEST, preferred_element_type=F32,
+    ones = jnp.ones((8, width), BF16)
+    total = sum(
+        lax.dot_general(ones, square, (((1,), (1,)), ((), ())), preferred_element_type=F32)
+        for square in halves_of(difference * difference)
     )
     return new, jnp.sqrt(total * (1.0 / width))
 

time: 62.5 us -> 62.4 us (level)
  no operation moved by 1% of the time
where the time goes in v5:
time: 62.4 us; the launch traced here: 62.1 us
  waiting for transfers between devices  32.5 us (52%)
  Pallas kernels  18.4 us (29%)
  starting transfers between devices  9.31 us (15%)
  local copies, waits for them, and re-layouts  1.09 us (2%)
  between operations  0.85 us (1%)
    ppermute x1, waiting for transfers between devices, shards(): got = lax.ppermute(mine, 'layer', partners)  13.1 us
    pallas_call x1, Pallas kernels, fine_jump(): pl.pallas_call(fine_kernel, in_specs=[in_place()] * 8, out_specs=[in_vmem...  12.4 us
    ppermute x6, waiting for transfers between devices, shards(): arrivals[c].append(lax.ppermute(carried[c], 'layer', route))  9.95 us
    ppermute x2, waiting for transfers between devices, shards(): received.append(lax.ppermute(sent[c], 'layer', partners))  5.45 us
    ppermute x6, starting transfers between devices, shards(): arrivals[c].append(lax.ppermute(carried[c], 'layer', route))  5.39 us
    ppermute x2, waiting for transfers between devices, shards(): returned.append(lax.ppermute(out, 'layer', partners))  3.95 us
    ppermute x2, starting transfers between devices, shards(): received.append(lax.ppermute(sent[c], 'layer', partners))  2.09 us
  transfers between devices with their start and end apart: 12, of which 7 were waited for; matrix products, arithmetic and copies ran while one was open for 0% of the time, Pallas kernels for 28%

profile of v5, /device:TPU:26, one launch (start us, length us, event | category | flops | bytes accessed | tf_op | source)
XLA Modules:
  0.0 62.1 jit_solution(5580733853742950433)
XLA Ops:
  0.6 1.1 %dynamic-slice_bitcast_fusion = f32[256,512]{1,0:T(8,128)S(1)} fusion(f32[1,512,512]{2,1,0:T(8,128)} %surrogate.1, s32[]{:T(128)S(6)} %select_n.11), kind=kLoop, calls=%fused_computation | loop fusion | bytes 1048580 | tf_op jit(solution)/shard_map/dynamic_slice | solution.py:389
  1.7 0.6 collective-permute-start.1
  2.3 13.1 %collective-permute-done.1.got = f32[256,512]{1,0:T(8,128)S(1)} collective-permute-done((f32[256,512]{1,0:T(8,128)S(1)}, f32[256,512]{1,0:T(8,128)S(1)}, u32[]{:S(2)}, u32[]{:S(2)}) %collective-permute-start.1) | collective-permute-done | bytes 524320 | tf_op jit(solution)/shard_map/ppermute | solution.py:390
  15.5 12.4 %shard_map.95 = (f32[64,512]{1,0:T(8,128)S(1)}, f32[64,512]{1,0:T(8,128)S(1)}, f32[64,512]{1,0:T(8,128)S(1)}, f32[64,512]{1,0:T(8,128)S(1)}, bf16[512,512]{1,0:T(8,128)(2,1)S(1)}, /*index=5*/bf16[512,512]{1,0:T(8,128)(2,1)S(1)}) custom-call(s32[2]{0:T(128)} %lengths.1, f32[1,256,512]{2,1,0:T(8,128)} %start.9, f32[1,512]{1,0:T(1,128)} %gain.1, ...), custom_call_target="tpu_custom_call" | custom-call | flops 6442450944 | bytes 6291456 | tf_op jit(solution)/shard_map/pallas_call | solution.py:171
  27.9 0.6 collective-permute-start.7
  28.5 1.5 %collective-permute-start = (f32[64,512]{1,0:T(8,128)S(1)}, f32[64,512]{1,0:T(8,128)S(1)}, u32[]{:S(2)}, u32[]{:S(2)}) collective-permute-start(f32[64,512]{1,0:T(8,128)S(1)} %get-tuple-element.23.jump), channel_id=1, source_target_pairs={{0,4},{4,0},{8,12},{12,8},{16,20},{20,16},{24,28},{28,24},{1,5},{5... | collective-permute-start | bytes 393224 | tf_op jit(solution)/shard_map/ppermute | solution.py:399
  30.3 4.1 %collective-permute-done.7.received = f32[64,512]{1,0:T(8,128)S(1)} collective-permute-done((f32[64,512]{1,0:T(8,128)S(1)}, f32[64,512]{1,0:T(8,128)S(1)}, u32[]{:S(2)}, u32[]{:S(2)}) %collective-permute-start.7) | collective-permute-done | bytes 131104 | tf_op jit(solution)/shard_map/ppermute | solution.py:399
  34.6 0.7 %collective-permute-start.8 = (f32[64,512]{1,0:T(8,128)S(1)}, f32[64,512]{1,0:T(8,128)S(1)}, u32[]{:S(2)}, u32[]{:S(2)}) collective-permute-start(f32[64,512]{1,0:T(8,128)S(1)} %shard_map.102.joined), channel_id=1, source_target_pairs={{0,8},{4,12},{1,9},{5,13},{2,10},{6,14},{3,11},{7,15}} | collective-permute-start | bytes 393224 | tf_op jit(solution)/shard_map/ppermute | solution.py:409
  35.3 1.4 %collective-permute-done.received = f32[64,512]{1,0:T(8,128)S(1)} collective-permute-done((f32[64,512]{1,0:T(8,128)S(1)}, f32[64,512]{1,0:T(8,128)S(1)}, u32[]{:S(2)}, u32[]{:S(2)}) %collective-permute-start) | collective-permute-done | bytes 131104 | tf_op jit(solution)/shard_map/ppermute | solution.py:399
  37.0 0.7 %collective-permute-start.3 = (f32[64,512]{1,0:T(8,128)S(1)}, f32[64,512]{1,0:T(8,128)S(1)}, u32[]{:S(2)}, u32[]{:S(2)}) collective-permute-start(f32[64,512]{1,0:T(8,128)S(1)} %shard_map.97.joined), channel_id=1, source_target_pairs={{0,8},{4,12},{1,9},{5,13},{2,10},{6,14},{3,11},{7,15}} | collective-permute-start | bytes 393224 | tf_op jit(solution)/shard_map/ppermute | solution.py:409
  37.7 1.2 %shard_map.98 = (bf16[512,512]{1,0:T(8,128)(2,1)S(1)}, bf16[512,512]{1,0:T(8,128)(2,1)S(1)}) custom-call(bf16[512,512]{1,0:T(8,128)(2,1)S(1)} %get-tuple-element.24.own_high, bf16[512,512]{1,0:T(8,128)(2,1)S(1)} %get-tuple-element.25.own_low, bf16[512,512]{1,0:T(8,128)(2,1)S(1)} %get-tuple-element.26.other_high, bf16[512,512]{1,0:T(8,128)(2,1)S(1)} %get-tuple-element.27.other_low), custom_call_target="tpu_custom_call" | custom-call | tf_op jit(solution)/shard_map/pallas_call | solution.py:240
  39.2 0.7 %collective-permute-start.9 = (f32[64,512]{1,0:T(8,128)S(1)}, f32[64,512]{1,0:T(8,128)S(1)}, u32[]{:S(2)}, u32[]{:S(2)}) collective-permute-start(f32[64,512]{1,0:T(8,128)S(1)} %shard_map.103), channel_id=1, source_target_pairs={{8,16},{12,20},{9,17},{13,21},{10,18},{14,22},{11,19},{15,23}} | collective-permute-start | bytes 393224 | tf_op jit(solution)/shard_map/ppermute | solution.py:409
  40.2 0.7 %collective-permute-start.4 = (f32[64,512]{1,0:T(8,128)S(1)}, f32[64,512]{1,0:T(8,128)S(1)}, u32[]{:S(2)}, u32[]{:S(2)}) collective-permute-start(f32[64,512]{1,0:T(8,128)S(1)} %shard_map.99), channel_id=1, source_target_pairs={{8,16},{12,20},{9,17},{13,21},{10,18},{14,22},{11,19},{15,23}} | collective-permute-start | bytes 393224 | tf_op jit(solution)/shard_map/ppermute | solution.py:409
  41.2 1.3 %collective-permute-start.10 = (f32[64,512]{1,0:T(8,128)S(1)}, f32[64,512]{1,0:T(8,128)S(1)}, u32[]{:S(2)}, u32[]{:S(2)}) collective-permute-start(f32[64,512]{1,0:T(8,128)S(1)} %shard_map.104), channel_id=1, source_target_pairs={{16,24},{20,28},{17,25},{21,29},{18,26},{22,30},{19,27},{23,31}} | collective-permute-start | bytes 393224 | tf_op jit(solution)/shard_map/ppermute | solution.py:409
  42.8 1.4 %collective-permute-start.5 = (f32[64,512]{1,0:T(8,128)S(1)}, f32[64,512]{1,0:T(8,128)S(1)}, u32[]{:S(2)}, u32[]{:S(2)}) collective-permute-start(f32[64,512]{1,0:T(8,128)S(1)} %shard_map.100), channel_id=1, source_target_pairs={{16,24},{20,28},{17,25},{21,29},{18,26},{22,30},{19,27},{23,31}} | collective-permute-start | bytes 393224 | tf_op jit(solution)/shard_map/ppermute | solution.py:409
  44.2 8.6 %collective-permute-done.10.arrivals_and_outs_2_ = f32[64,512]{1,0:T(8,128)S(1)} collective-permute-done((f32[64,512]{1,0:T(8,128)S(1)}, f32[64,512]{1,0:T(8,128)S(1)}, u32[]{:S(2)}, u32[]{:S(2)}) %collective-permute-start.10) | collective-permute-done | bytes 131104 | tf_op jit(solution)/shard_map/ppermute | solution.py:409
  53.2 0.6 collective-permute-start.11
  53.8 1.3 %collective-permute-done.5.arrivals_and_outs_2_ = f32[64,512]{1,0:T(8,128)S(1)} collective-permute-done((f32[64,512]{1,0:T(8,128)S(1)}, f32[64,512]{1,0:T(8,128)S(1)}, u32[]{:S(2)}, u32[]{:S(2)}) %collective-permute-start.5) | collective-permute-done | bytes 131104 | tf_op jit(solution)/shard_map/ppermute | solution.py:409
  55.4 0.6 collective-permute-start.6
  56.4 0.3 shard_map.106
  56.7 2.5 %collective-permute-done.11.ahead = f32[64,512]{1,0:T(8,128)S(1)} collective-permute-done((f32[64,512]{1,0:T(8,128)S(1)}, f32[64,512]{1,0:T(8,128)S(1)}, u32[]{:S(2)}, u32[]{:S(2)}) %collective-permute-start.11) | collective-permute-done | bytes 131104 | tf_op jit(solution)/shard_map/ppermute | solution.py:416
  59.2 0.3 shard_map.107
  59.6 1.4 %collective-permute-done.6.ahead = f32[64,512]{1,0:T(8,128)S(1)} collective-permute-done((f32[64,512]{1,0:T(8,128)S(1)}, f32[64,512]{1,0:T(8,128)S(1)}, u32[]{:S(2)}, u32[]{:S(2)}) %collective-permute-start.6) | collective-permute-done | bytes 131104 | tf_op jit(solution)/shard_map/ppermute | solution.py:416
  61.0 1.1 %shard_map.109 = (f32[1,256,512]{2,1,0:T(8,128)}, f32[1,256]{1,0:T(1,128)}) custom-call(f32[64,512]{1,0:T(8,128)S(1)} %collective-permute-done.6.ahead, f32[64,512]{1,0:T(8,128)S(1)} %get-tuple-element.23.jump, f32[1,256,512]{2,1,0:T(8,128)S(1)} %copy-done, bf16[512,512]{1,0:T(8,128)(2,1)S(1)} %get-tuple-element.24.own_high, ...), custom_call_target="tpu_custom_call" | custom-call | tf_op jit(solution)/shard_map/pallas_call | solution.py:370
  (18 shorter events, 3.0 us)
Async XLA Ops:
  1.7 13.7 %collective-permute-start.1 = (f32[256,512]{1,0:T(8,128)S(1)}, f32[256,512]{1,0:T(8,128)S(1)}, u32[]{:S(2)}, u32[]{:S(2)}) collective-permute-start(f32[256,512]{1,0:T(8,128)S(1)} %dynamic-slice_bitcast_fusion), channel_id=1, source_target_pairs={{0,4},{4,0},{8,12},{12,8},{16,20},{20,16},{24,28},{28,24},{1,5},{5... | collective-permute-start | bytes 1572872 | tf_op jit(solution)/shard_map/ppermute | solution.py:390
  15.5 14.5 %collective-permute-start.2 = (f32[256,512]{1,0:T(8,128)S(1)}, f32[256,512]{1,0:T(8,128)S(1)}, u32[]{:S(2)}, u32[]{:S(2)}) collective-permute-start(f32[256,512]{1,0:T(8,128)S(1)} %collective-permute-done.1.got), channel_id=1, source_target_pairs={{0,1},{1,0},{2,3},{3,2},{4,5},{5,4},{6,7},{7,6},{8,9},{9,8},{10,11... | collective-permute-start | bytes 1572872 | tf_op jit(solution)/shard_map/ppermute | solution.py:400
  27.9 6.4 %collective-permute-start.7 = (f32[64,512]{1,0:T(8,128)S(1)}, f32[64,512]{1,0:T(8,128)S(1)}, u32[]{:S(2)}, u32[]{:S(2)}) collective-permute-start(f32[64,512]{1,0:T(8,128)S(1)} %get-tuple-element.32.jump), channel_id=1, source_target_pairs={{0,4},{4,0},{8,12},{12,8},{16,20},{20,16},{24,28},{28,24},{1,5},{5... | collective-permute-start | bytes 393224 | tf_op jit(solution)/shard_map/ppermute | solution.py:399
  28.5 8.2 %collective-permute-start = (f32[64,512]{1,0:T(8,128)S(1)}, f32[64,512]{1,0:T(8,128)S(1)}, u32[]{:S(2)}, u32[]{:S(2)}) collective-permute-start(f32[64,512]{1,0:T(8,128)S(1)} %get-tuple-element.23.jump), channel_id=1, source_target_pairs={{0,4},{4,0},{8,12},{12,8},{16,20},{20,16},{24,28},{28,24},{1,5},{5... | collective-permute-start | bytes 393224 | tf_op jit(solution)/shard_map/ppermute | solution.py:399
  34.6 4.3 %collective-permute-start.8 = (f32[64,512]{1,0:T(8,128)S(1)}, f32[64,512]{1,0:T(8,128)S(1)}, u32[]{:S(2)}, u32[]{:S(2)}) collective-permute-start(f32[64,512]{1,0:T(8,128)S(1)} %shard_map.102.joined), channel_id=1, source_target_pairs={{0,8},{4,12},{1,9},{5,13},{2,10},{6,14},{3,11},{7,15}} | collective-permute-start | bytes 393224 | tf_op jit(solution)/shard_map/ppermute | solution.py:409
  37.0 2.9 %collective-permute-start.3 = (f32[64,512]{1,0:T(8,128)S(1)}, f32[64,512]{1,0:T(8,128)S(1)}, u32[]{:S(2)}, u32[]{:S(2)}) collective-permute-start(f32[64,512]{1,0:T(8,128)S(1)} %shard_map.97.joined), channel_id=1, source_target_pairs={{0,8},{4,12},{1,9},{5,13},{2,10},{6,14},{3,11},{7,15}} | collective-permute-start | bytes 393224 | tf_op jit(solution)/shard_map/ppermute | solution.py:409
  39.2 1.7 %collective-permute-start.9 = (f32[64,512]{1,0:T(8,128)S(1)}, f32[64,512]{1,0:T(8,128)S(1)}, u32[]{:S(2)}, u32[]{:S(2)}) collective-permute-start(f32[64,512]{1,0:T(8,128)S(1)} %shard_map.103), channel_id=1, source_target_pairs={{8,16},{12,20},{9,17},{13,21},{10,18},{14,22},{11,19},{15,23}} | collective-permute-start | bytes 393224 | tf_op jit(solution)/shard_map/ppermute | solution.py:409
  40.2 2.3 %collective-permute-start.4 = (f32[64,512]{1,0:T(8,128)S(1)}, f32[64,512]{1,0:T(8,128)S(1)}, u32[]{:S(2)}, u32[]{:S(2)}) collective-permute-start(f32[64,512]{1,0:T(8,128)S(1)} %shard_map.99), channel_id=1, source_target_pairs={{8,16},{12,20},{9,17},{13,21},{10,18},{14,22},{11,19},{15,23}} | collective-permute-start | bytes 393224 | tf_op jit(solution)/shard_map/ppermute | solution.py:409
  41.2 11.7 %collective-permute-start.10 = (f32[64,512]{1,0:T(8,128)S(1)}, f32[64,512]{1,0:T(8,128)S(1)}, u32[]{:S(2)}, u32[]{:S(2)}) collective-permute-start(f32[64,512]{1,0:T(8,128)S(1)} %shard_map.104), channel_id=1, source_target_pairs={{16,24},{20,28},{17,25},{21,29},{18,26},{22,30},{19,27},{23,31}} | collective-permute-start | bytes 393224 | tf_op jit(solution)/shard_map/ppermute | solution.py:409
  42.8 13.3 %copy-start = (f32[1,256,512]{2,1,0:T(8,128)S(1)}, f32[1,256,512]{2,1,0:T(8,128)}, u32[]{:S(2)}) copy-start(f32[1,256,512]{2,1,0:T(8,128)} %start.9) | copy-start | bytes 1572868
  42.8 12.3 %collective-permute-start.5 = (f32[64,512]{1,0:T(8,128)S(1)}, f32[64,512]{1,0:T(8,128)S(1)}, u32[]{:S(2)}, u32[]{:S(2)}) collective-permute-start(f32[64,512]{1,0:T(8,128)S(1)} %shard_map.100), channel_id=1, source_target_pairs={{16,24},{20,28},{17,25},{21,29},{18,26},{22,30},{19,27},{23,31}} | collective-permute-start | bytes 393224 | tf_op jit(solution)/shard_map/ppermute | solution.py:409
  53.2 6.1 %collective-permute-start.11 = (f32[64,512]{1,0:T(8,128)S(1)}, f32[64,512]{1,0:T(8,128)S(1)}, u32[]{:S(2)}, u32[]{:S(2)}) collective-permute-start(f32[64,512]{1,0:T(8,128)S(1)} %get-tuple-element.36), channel_id=1, source_target_pairs={{0,4},{4,0},{8,12},{12,8},{16,20},{20,16},{24,28},{28,24},{1,5},{5... | collective-permute-start | bytes 393224 | tf_op jit(solution)/shard_map/ppermute | solution.py:416
  55.4 5.6 %collective-permute-start.6 = (f32[64,512]{1,0:T(8,128)S(1)}, f32[64,512]{1,0:T(8,128)S(1)}, u32[]{:S(2)}, u32[]{:S(2)}) collective-permute-start(f32[64,512]{1,0:T(8,128)S(1)} %get-tuple-element.30), channel_id=1, source_target_pairs={{0,4},{4,0},{8,12},{12,8},{16,20},{20,16},{24,28},{28,24},{1,5},{5... | collective-permute-start | bytes 393224 | tf_op jit(solution)/shard_map/ppermute | solution.py:416
